TPU v7x, 32 devices: a whole 2x2x4 slice. The times are simulated.
32 devices in a mesh: own: 8 (over z, core), help: 4 (over y, x).
Axes of the slice: x: 2, y: 2, z: 4, core: 2. Of those that a mesh axis runs over, the one named last changes fastest.
Arguments:
- records: bfloat16 [16384, 256], P(('own', 'help')), may hold values from -6 to 6
- owner: int32 [16384, 1], P(('own', 'help')), may hold values from 0 to 7; in each aligned block of 512 rows (0 to 511, 512 to 1023, ...) at most 128 rows name the same one
- subkey: int32 [16384], P(('own', 'help')), may hold values from 0 to 3
- source: int32 [16384], P(('own', 'help')), may hold values from 0 to 3
Outputs:
- resolved: bfloat16 [16384, 256], P(('own', 'help'))
Inputs may be any that keep to these rules, and one draw needn't show every extreme that they name: Among the 512 records of one device (aligned blocks of rows), no owner is named more than 128 times, and in every draw some device names some owner exactly 128 times.
All inputs are finite; a program needn't handle non-finite values.
Results may differ from a plain program's by a relative error of at most 0.0052.
Values may be sent and summed in bfloat16 or wider, within the bound.
No kernel may reach another device: no remote copies, remote signals or barrier semaphores. Data moves between devices by JAX's collectives and lax.ppermute only.
A program may use at most 192 MiB of HBM per device.

v0:
```python
import jax
import jax.numpy as jnp
from jax import lax
from jax.sharding import PartitionSpec as P

SOURCES = 4


epsilon = 1e-06
sharpness = 4.0


def normalized(records):
    values_f = records.astype(jnp.float32)
    inverse = lax.rsqrt(jnp.mean(values_f * values_f, axis=1, keepdims=True) + epsilon)
    return (values_f * inverse).astype(jnp.bfloat16)


def pair_weights(query_rows, query_codes, key_rows, key_codes):
    scores = lax.dot_general(
        query_rows, key_rows, (((1,), (1,)), ((), ())), preferred_element_type=jnp.float32
    )
    matched = (query_codes[:, None] >= 0) & (key_codes[None, :] >= 0)
    matched = matched & (query_codes[:, None] // SOURCES == key_codes[None, :] // SOURCES)
    matched = matched & (query_codes[:, None] % SOURCES != key_codes[None, :] % SOURCES)
    return jnp.where(
        matched, jnp.exp(scores * (sharpness / query_rows.shape[1])), jnp.zeros_like(scores)
    )


def resolve(held_rows, partner, mass):
    merged = held_rows.astype(jnp.float32) + partner * lax.rsqrt(1.0 + mass)[:, None]
    return merged.astype(jnp.bfloat16)


def shards(records, owner, subkey, source):
    row_count = records.shape[0]
    width = records.shape[1]
    owners = lax.axis_size("own")
    slot_count = 2 * row_count
    capacity = slot_count // owners
    scaled = normalized(records)
    target = owner[:, 0]
    onehot = (target[:, None] == jnp.arange(owners, dtype=jnp.int32)[None, :]).astype(jnp.int32)
    slot_rank = jnp.sum(jnp.cumsum(onehot, axis=0) * onehot, axis=1) - 1
    slot_index = target * capacity + slot_rank
    outbox = jnp.zeros((slot_count, width), jnp.bfloat16).at[slot_index].set(scaled)
    out_codes = jnp.full((slot_count,), -1, jnp.int32).at[slot_index].set(subkey * SOURCES + source)
    inbox, in_codes = (
        lax.all_to_all(
            outbox.reshape(owners, capacity, width), "own", split_axis=0, concat_axis=0, tiled=True
        ),
        lax.all_to_all(
            out_codes.reshape(owners, capacity), "own", split_axis=0, concat_axis=0, tiled=True
        ),
    )
    held_rows = inbox.reshape(slot_count, width)
    held_codes = in_codes.reshape(slot_count)
    incoming = (
        lax.all_gather(held_rows, "help", axis=0, tiled=True),
        lax.all_gather(held_codes, "help", axis=0, tiled=True),
    )
    weight = pair_weights(held_rows, held_codes, incoming[0], incoming[1])
    partner_next = jnp.dot(
        weight.astype(jnp.bfloat16), incoming[0], preferred_element_type=jnp.float32
    )
    mass = jnp.sum(weight, axis=1)
    merged = resolve(held_rows, partner_next, mass).reshape(owners, capacity, width)
    returned = lax.all_to_all(merged, "own", split_axis=0, concat_axis=0, tiled=True).reshape(
        slot_count, width
    )
    return returned[slot_index]


def solution(mesh):
    return jax.shard_map(
        shards,
        mesh=mesh,
        in_specs=(
            P(("own", "help"), None),
            P(("own", "help"), None),
            P(("own", "help")),
            P(("own", "help")),
        ),
        out_specs=P(("own", "help"), None),
        check_vma=False,
    )
```

profile of v0, /device:TPU:0, one launch (start us, length us, event | category | flops | bytes accessed | tf_op | source)
XLA Modules:
  0.0 117.5 jit_solution(4763169931657767500)
XLA Ops:
  6.5 0.0 all-gather.2.cloned.1.call-start
  6.5 0.7 fusion.20
  7.2 1.1 reduce-window.6
  8.4 0.2 slice_reduce_fusion
  8.6 0.8 fusion.19
  9.4 0.7 compare_select_fusion
  10.1 1.1 fusion.13
  11.2 3.0 %scatter_custom_fusion = bf16[1024,256]{1,0:T(8,128)(2,1)S(1)} fusion(s32[512]{0:T(512)S(1)} %bitcast.30, bf16[512,256]{1,0:T(8,128)(2,1)} %param.4, f32[512]{0:T(512)S(1)} %add_rsqrt_fusion.1, bf16[]{:T(256)} %constant.61.clone.1), kind=kCustom, calls=%fused_computation.14 | custom fusion | flops 393216 | bytes 788482 | tf_op jit(solution)/shard_map/scatter | solution.py:47
  14.2 21.6 %all_to_all.19 = bf16[8,128,256]{2,1,0:T(8,128)(2,1)} all-to-all(bf16[8,128,256]{2,1,0:T(8,128)(2,1)S(1)} %bitcast.23), channel_id=1, replica_groups=mesh['own'=8,'help'=4] {'own'}, dimensions={0} | all-to-all | bytes 1048576 | tf_op jit(solution)/shard_map/all_to_all | solution.py:50
  35.8 0.0 all-gather.2.cloned.1.call-update
  35.8 0.7 multiply_add_fusion
  36.5 2.4 %scatter_custom_fusion.1 = s32[1024]{0:T(1024)S(1)} fusion(s32[512]{0:T(512)S(1)} %bitcast.31, s32[512]{0:T(512)S(1)} %multiply_add_fusion, s32[]{:T(128)} %constant.64.clone.1), kind=kCustom, calls=%fused_computation.45 | custom fusion | bytes 4100 | tf_op jit(solution)/shard_map/scatter | solution.py:48
  38.9 7.9 %all_to_all.20 = s32[8,1,128]{2,1,0:T(1,128)S(1)} all-to-all(s32[8,1,128]{2,1,0:T(1,128)S(1)} %bitcast.29), channel_id=1, replica_groups=mesh['own'=8,'help'=4] {'own'}, dimensions={0} | all-to-all | bytes 8192 | tf_op jit(solution)/shard_map/all_to_all | solution.py:53
  46.9 8.3 %all_gather.6 = s32[4096]{0:T(1024)S(1)} all-gather(s32[1024]{0:T(1024)S(1)} %bitcast.24), channel_id=1, replica_groups=mesh['own'=8,'help'=4] {'help'}, dimensions={0}, use_global_device_ids=true | all-gather | bytes 20480 | tf_op jit(solution)/shard_map/all_gather | solution.py:61
  55.3 15.0 %all-gather.2.cloned.1.call-done = bf16[4096,256]{1,0:T(8,128)(2,1)} async-done(((bf16[1024,256]{1,0:T(8,128)(2,1)}), bf16[4096,256]{1,0:T(8,128)(2,1)}) %all-gather.2.cloned.1.call-update) | async-done | bytes 2097168 | tf_op jit(solution)/shard_map/all_gather | solution.py:60
  70.3 0.0 copy-start
  70.3 0.0 copy-start.1
  70.3 9.7 %fusion = (f32[1024]{0:T(1024)S(1)}, f32[1024,4096]{1,0:T(8,128)S(1)}) fusion(s32[4096]{0:T(1024)S(1)} %get-tuple-element.6, s32[4096]{0:T(1024)S(1)} %get-tuple-element.5, s32[1024]{0:T(1024)S(1)} %get-tuple-element.8, s32[1024]{0:T(1024)S(1)} %get-tuple-element.7, pred[4096]{0:T(1024)(128)(4,1)S(1)} %broadcast_compare_fusion, ...), kind=kOutput, calls=%fused_computation.4 | convolution fusion | flops 2181037056 | bytes 19448832 | tf_op jit(solution)/shard_map/dot_general | solution.py:20
  80.0 0.0 copy-done
  80.0 0.0 copy-done.1
  80.0 8.1 %fusion.10 = bf16[1024,256]{1,0:T(8,128)(2,1)} fusion(bf16[4096,256]{1,0:T(8,128)(2,1)S(1)} %copy-done.1, f32[1024,4096]{1,0:T(8,128)S(1)} %get-tuple-element.10, s32[4096]{0:T(1024)S(1)} %get-tuple-element.6, s32[4096]{0:T(1024)S(1)} %get-tuple-element.5, s32[1024]{0:T(1024)S(1)} %get-tuple-element.8, s32[1024]{0:T(1024)S(1)} %get-tuple-element.7, ...), kind=kOutput, calls=%fused_computation.9 | convolution fusion | flops 2182086656 | bytes 19973120 | tf_op jit(solution)/shard_map/dot_general | solution.py:64
  88.2 4.6 %all-to-all-start.2 = ((bf16[8,128,256]{2,1,0:T(8,128)(2,1)}), bf16[8,128,256]{2,1,0:T(8,128)(2,1)S(1)}, u32[]{:S(2)}, u32[]{:S(2)}) async-start(bf16[8,128,256]{2,1,0:T(8,128)(2,1)} %bitcast.10), calls=%async_computation.2 | async-start | bytes 1048576 | tf_op jit(solution)/shard_map/all_to_all | solution.py:69
  92.8 15.4 %all-to-all-done.2 = bf16[8,128,256]{2,1,0:T(8,128)(2,1)S(1)} async-done(((bf16[8,128,256]{2,1,0:T(8,128)(2,1)}), bf16[8,128,256]{2,1,0:T(8,128)(2,1)S(1)}, u32[]{:S(2)}, u32[]{:S(2)}) %all-to-all-start.2) | async-done | bytes 524320 | tf_op jit(solution)/shard_map/all_to_all | solution.py:69
  108.1 2.6 %gather_fusion = bf16[512,256]{1,0:T(8,128)(2,1)} fusion(bf16[1024,256]{1,0:T(8,128)(2,1)S(1)} %bitcast.19, s32[1024]{0:T(1024)S(1)} %pad_clamp_fusion), kind=kCustom, calls=%fused_computation | custom fusion | bytes 526336 | tf_op jit(solution)/shard_map/gather | solution.py:72
  (10 shorter events, 0.1 us)
Async XLA Ops:
  6.5 63.7 %all-gather.2.cloned.1.call-start = ((), (), s32[]{:S(2)}) async-start(), calls=%async_computation.3 | async-start | bytes 2621440 | tf_op jit(solution)/shard_map/all_gather | solution.py:60
  70.3 9.7 %copy-start = (bf16[8,128,256]{2,1,0:T(8,128)(2,1)S(1)}, bf16[8,128,256]{2,1,0:T(8,128)(2,1)}, u32[]{:S(2)}) copy-start(bf16[8,128,256]{2,1,0:T(8,128)(2,1)} %all_to_all.19) | copy-start | bytes 1572868
  70.3 9.7 %copy-start.1 = (bf16[4096,256]{1,0:T(8,128)(2,1)S(1)}, bf16[4096,256]{1,0:T(8,128)(2,1)}, u32[]{:S(2)}) copy-start(bf16[4096,256]{1,0:T(8,128)(2,1)} %all-gather.2.cloned.1.call-done) | copy-start | bytes 6291460
  88.2 20.0 %all-to-all-start.2 = ((bf16[8,128,256]{2,1,0:T(8,128)(2,1)}), bf16[8,128,256]{2,1,0:T(8,128)(2,1)S(1)}, u32[]{:S(2)}, u32[]{:S(2)}) async-start(bf16[8,128,256]{2,1,0:T(8,128)(2,1)} %bitcast.10), calls=%async_computation.2 | async-start | bytes 1048576 | tf_op jit(solution)/shard_map/all_to_all | solution.py:69
Sparse Core Ops, SparseCore 0:
  35.9 34.2 all-gather.1
where the time goes:
time: 118 us
  blocking collectives  37.8 us (32%)
  waiting for transfers between devices  30.4 us (26%)
  matrix products  17.9 us (15%)
  between operations  13.5 us (11%)
  other arithmetic  8.15 us (7%)
  local copies, waits for them, and re-layouts  5.24 us (4%)
  starting transfers between devices  4.61 us (4%)
    all_to_all x1, blocking collectives, shards(): lax.all_to_all(outbox.reshape(owners, capacity, width), 'own', split_axis...  21.6 us
    all_to_all x1, waiting for transfers between devices, shards(): lax.all_to_all(merged, 'own', split_axis=0, concat_axis=0, tiled=True)  15.4 us
    all_gather x1, waiting for transfers between devices, shards(): lax.all_gather(held_rows, 'help', axis=0, tiled=True)  15 us
    dot_general x1, matrix products, pair_weights(): lax.dot_general(query_rows, key_rows, (((1,), (1,)), ((), ())), preferred...  9.72 us
    all_gather x1, blocking collectives, shards(): lax.all_gather(held_codes, 'help', axis=0, tiled=True)  8.34 us
    dot_general x1, matrix products, shards(): jnp.dot(weight.astype(jnp.bfloat16), incoming[0], preferred_element_type=...  8.14 us
    all_to_all x1, blocking collectives, shards(): lax.all_to_all(out_codes.reshape(owners, capacity), 'own', split_axis=0,...  7.92 us
    all_to_all x1, starting transfers between devices, shards(): lax.all_to_all(merged, 'own', split_axis=0, concat_axis=0, tiled=True)  4.61 us
  transfers between devices with their start and end apart: 2, of which 2 were waited for; matrix products, arithmetic and copies ran while one was open for 3% of the time, Pallas kernels for 0%

commit v1 on v0

v1 whole, which is shorter than its diff:
```python
import functools

import jax
import jax.numpy as jnp
from jax import lax
from jax.experimental import pallas as pl
from jax.experimental.pallas import tpu as pltpu
from jax.sharding import Mesh, PartitionSpec as P

SUBKEYS = 4
SOURCES = 4
CODES = SUBKEYS * SOURCES
EPSILON = 1e-06
SHARPNESS = 4.0
LOG2E = 1.4426950408889634
PAD = 8
SWAP = [(0, 1), (1, 0)]
NT = (((1,), (1,)), ((), ()))
VMEM_LIMIT = 48 * 2**20


def selections(full_codes, owner_of, count, cap):
    rows = full_codes.shape[1]
    lines = max(8, count)
    line = lax.broadcasted_iota(jnp.int32, (lines, rows), 0)
    wanted = jnp.full((lines, rows), -1, jnp.int32)
    for j in range(count):
        wanted = jnp.where(line == j, owner_of(j), wanted)
    named = wanted == jnp.broadcast_to(full_codes // CODES, (lines, rows))
    before = lax.broadcasted_iota(jnp.int32, (rows, rows), 0)
    after = lax.broadcasted_iota(jnp.int32, (rows, rows), 1)
    earlier = jnp.where(before < after, 1.0, 0.0).astype(jnp.bfloat16)
    rank = jnp.dot(
        jnp.where(named, 1.0, 0.0).astype(jnp.bfloat16),
        earlier,
        preferred_element_type=jnp.float32,
    )
    rank = jnp.where(named, rank, -1.0).astype(jnp.int32)
    slot = lax.broadcasted_iota(jnp.int32, (cap, rows), 0)
    return [
        jnp.where(slot == rank[j : j + 1, :], 1.0, 0.0).astype(jnp.bfloat16)
        for j in range(count)
    ]


def scale_kernel(rows_ref, owner_ref, subkey_ref, source_ref, out_ref):
    rows, width = rows_ref.shape
    values = rows_ref[...].astype(jnp.float32)
    inverse = lax.rsqrt(jnp.mean(values * values, axis=1, keepdims=True) + EPSILON)
    out_ref[:rows, :] = (values * inverse).astype(jnp.bfloat16)
    codes = (owner_ref[...] * SUBKEYS + subkey_ref[...]) * SOURCES + source_ref[...]
    line = lax.broadcasted_iota(jnp.int32, (PAD, width), 0)
    lines = jnp.zeros((PAD, width), jnp.int32)
    for k in range(rows // width):
        lines = jnp.where(line == k, codes[:, k * width : (k + 1) * width], lines)
    out_ref[rows:, :] = lines.astype(jnp.float32).astype(jnp.bfloat16)


def scale(records, owner, subkey, source):
    rows, width = records.shape
    return pl.pallas_call(
        scale_kernel,
        out_shape=jax.ShapeDtypeStruct((rows + PAD, width), jnp.bfloat16),
        compiler_params=pltpu.CompilerParams(vmem_limit_bytes=VMEM_LIMIT),
    )(records, owner.reshape(1, rows), subkey.reshape(1, rows), source.reshape(1, rows))


def pack_kernel(count, cap, owners_ref, *refs):
    blocks, messages = refs[:2], refs[2:]
    for part in range(2):
        width = blocks[part].shape[1]
        rows = blocks[part].shape[0] - PAD
        scaled = blocks[part][:rows, :]
        lines = blocks[part][rows:, :].astype(jnp.float32)
        full_codes = jnp.concatenate(
            [lines[k : k + 1, :] for k in range(rows // width)], axis=1
        ).astype(jnp.int32)
        codes = jnp.broadcast_to(full_codes % CODES + 1, (8, rows))
        codes = codes.astype(jnp.float32).astype(jnp.bfloat16)
        picks = selections(full_codes, lambda j: owners_ref[0, j], count, cap)
        for j in range(count):
            picked = jnp.dot(picks[j], scaled, preferred_element_type=jnp.float32)
            messages[j][part, :cap, :] = picked.astype(jnp.bfloat16)
            line = lax.dot_general(codes, picks[j], NT, preferred_element_type=jnp.float32)
            messages[j][part, cap:, :] = jnp.zeros((PAD, width), jnp.bfloat16)
            messages[j][part, cap:, :cap] = line.astype(jnp.bfloat16)


def pack(owners, blocks, count, cap):
    shape = jax.ShapeDtypeStruct((2, cap + PAD, blocks[0].shape[1]), jnp.bfloat16)
    return pl.pallas_call(
        functools.partial(pack_kernel, count, cap),
        in_specs=[pl.BlockSpec(memory_space=pltpu.SMEM)]
        + [pl.BlockSpec(memory_space=pltpu.VMEM)] * 2,
        out_specs=[pl.BlockSpec(memory_space=pltpu.VMEM)] * count,
        out_shape=[shape] * count,
        compiler_params=pltpu.CompilerParams(vmem_limit_bytes=VMEM_LIMIT),
    )(owners, *blocks)


def place_kernel(count, cap, owners_ref, owner_ref, out_ref):
    rows = owner_ref.shape[0]
    owner = owner_ref[...]
    lane = lax.broadcasted_iota(jnp.int32, (rows, 128), 1)
    named = owner == lane
    later = lax.broadcasted_iota(jnp.int32, (rows, rows), 0)
    before = lax.broadcasted_iota(jnp.int32, (rows, rows), 1)
    earlier = jnp.where(before < later, 1.0, 0.0).astype(jnp.bfloat16)
    rank = jnp.dot(
        earlier,
        jnp.where(named, 1.0, 0.0).astype(jnp.bfloat16),
        preferred_element_type=jnp.float32,
    )
    rank = jnp.sum(jnp.where(named, rank, 0.0), axis=1, keepdims=True).astype(jnp.int32)
    for i in range(2 * count):
        rank = rank + jnp.where(owner == owners_ref[i // count, i % count], i * cap, 0)
    out_ref[...] = rank


def place(owners, owner, count, cap):
    return pl.pallas_call(
        functools.partial(place_kernel, count, cap),
        in_specs=[
            pl.BlockSpec(memory_space=pltpu.SMEM),
            pl.BlockSpec(memory_space=pltpu.VMEM),
        ],
        out_specs=pl.BlockSpec(memory_space=pltpu.VMEM),
        out_shape=jax.ShapeDtypeStruct(owner.shape, jnp.int32),
        compiler_params=pltpu.CompilerParams(vmem_limit_bytes=VMEM_LIMIT),
    )(owners, owner)


def code_line(ref, part, cap):
    return ref[part, cap : cap + 8, :cap].astype(jnp.float32)[0:1, :].astype(jnp.int32) - 1


def match_kernel(queries, cap, last, *refs):
    outs = refs[-queries:] if last else refs[-2:]
    refs = refs[: -queries] if last else refs[:-2]
    held, refs = refs[:queries], refs[queries:]
    sums, keys = (refs[:2], refs[2:]) if last else (None, refs)
    width = held[0].shape[2]
    diagonal = lax.broadcasted_iota(jnp.int32, (cap, cap), 0) == lax.broadcasted_iota(
        jnp.int32, (cap, cap), 1
    )
    for j in range(queries):
        query = held[j][:, :cap, :].reshape(2 * cap, width)
        span = slice(j * 2 * cap, (j + 1) * 2 * cap)
        columns = []
        for part in range(2):
            line = jnp.broadcast_to(code_line(held[j], part, cap), (cap, cap))
            picked = jnp.where(diagonal, line, 0).astype(jnp.float32)
            columns.append(jnp.sum(picked, axis=1, keepdims=True))
        query_codes = jnp.concatenate(columns, axis=0).astype(jnp.int32)

        def add(key_ref, first, carry):
            total, mass = carry
            pair = key_ref.at[pl.ds(first, 2)]
            key = pair[:, :cap, :].reshape(2 * cap, width)
            key_codes = jnp.concatenate([code_line(pair, k, cap) for k in range(2)], axis=1)
            score = lax.dot_general(query, key, NT, preferred_element_type=jnp.float32)
            differ = query_codes ^ key_codes
            matched = (differ >= 1) & (differ < SOURCES)
            weight = jnp.where(matched, jnp.exp2(score * (SHARPNESS / width * LOG2E)), 0.0)
            mass = mass + jnp.sum(weight, axis=1, keepdims=True)
            return total + jnp.dot(
                weight.astype(jnp.bfloat16), key, preferred_element_type=jnp.float32
            ), mass

        if last:
            carry = sums[0][span, :], sums[1][span, :]
        else:
            carry = jnp.zeros((2 * cap, width), jnp.float32), jnp.zeros((2 * cap, 1), jnp.float32)
        for key_ref in keys:
            pairs = key_ref.shape[0] // 2
            if pairs == 1:
                carry = add(key_ref, 0, carry)
            else:
                carry = lax.fori_loop(
                    0, pairs, lambda i, c, key_ref=key_ref: add(key_ref, 2 * i, c), carry
                )
        total, mass = carry
        if last:
            merged = query.astype(jnp.float32) + total * lax.rsqrt(1.0 + mass)
            outs[j][...] = merged.astype(jnp.bfloat16).reshape(2, cap, width)
        else:
            outs[0][span, :] = total
            outs[1][span, :] = mass


def match(held, keys, cap, sums=None):
    count, width = len(held), held[0].shape[2]
    if sums is None:
        shapes = [
            jax.ShapeDtypeStruct((count * 2 * cap, width), jnp.float32),
            jax.ShapeDtypeStruct((count * 2 * cap, 1), jnp.float32),
        ]
    else:
        shapes = [jax.ShapeDtypeStruct((2, cap, width), jnp.bfloat16)] * count
    operands = (*held, *(sums or ()), *keys)
    return pl.pallas_call(
        functools.partial(match_kernel, count, cap, sums is not None),
        in_specs=[pl.BlockSpec(memory_space=pltpu.VMEM)] * len(operands),
        out_specs=[pl.BlockSpec(memory_space=pltpu.VMEM)] * len(shapes),
        out_shape=shapes,
        compiler_params=pltpu.CompilerParams(vmem_limit_bytes=VMEM_LIMIT),
    )(*operands)


def unpack_kernel(count, cap, place_ref, *refs):
    mine, sibling, out_ref = refs[:count], refs[count : 2 * count], refs[-1]
    rows = out_ref.shape[0]
    slot = lax.broadcasted_iota(jnp.int32, (rows, 2 * count * cap), 1)
    picks = jnp.where(slot == place_ref[...], 1.0, 0.0).astype(jnp.bfloat16)
    blocks = [m[0] for m in mine] + [m[1] for m in sibling]
    out_ref[...] = jnp.dot(
        picks, jnp.concatenate(blocks, axis=0), preferred_element_type=jnp.float32
    ).astype(jnp.bfloat16)


def unpack(places, mine, sibling, cap):
    count, width = len(mine), mine[0].shape[2]
    return pl.pallas_call(
        functools.partial(unpack_kernel, count, cap),
        in_specs=[pl.BlockSpec(memory_space=pltpu.VMEM)] * (2 * count + 1),
        out_specs=pl.BlockSpec(memory_space=pltpu.VMEM),
        out_shape=jax.ShapeDtypeStruct((places.shape[0], width), jnp.bfloat16),
        compiler_params=pltpu.CompilerParams(vmem_limit_bytes=VMEM_LIMIT),
    )(places, *mine, *sibling)


def shards(records, owner, subkey, source):
    row_count = records.shape[0]
    chips = lax.axis_size("z_lo") * lax.axis_size("near")
    near, rest = lax.axis_size("near"), lax.axis_size("far")
    cap = 2 * row_count // chips
    count = chips // 2
    by_hops = sorted(range(chips), key=lambda d: -d.bit_count())
    flips = [[d for d in by_hops if d.bit_count() % 2 == odd] for odd in (1, 0)]
    core = lax.axis_index("core")
    spot = lax.axis_index(("z_lo", "near"))
    table = jnp.array(flips, jnp.int32)
    owners = spot ^ jnp.where(core == 0, table, table[::-1])

    def to_core(x):
        return lax.ppermute(x, "core", SWAP)

    def to_half(x):
        return lax.ppermute(x, "z_hi", SWAP)

    def to_chip(x, j):
        def number(c, s):
            return (s // near * 2 + c) * near + s % near

        pairs = [
            (number(c, s), number(c, s ^ flips[c][j])) for c in range(2) for s in range(chips)
        ]
        return lax.ppermute(x, ("z_lo", "core", "near"), pairs)

    def spread(blocks):
        messages = [to_chip(m, j) for j, m in enumerate(pack(owners, blocks, count, cap))]
        keys = messages
        if rest > 1:
            keys = [lax.all_gather(m, "far", axis=0, tiled=True) for m in messages]
        return messages, keys + [to_core(m) for m in keys]

    block = scale(records, owner, subkey, source)
    far_block = to_half(block)
    held, keys = spread((block, to_core(block)))
    sums = match(held, keys, cap)
    _, far_keys = spread((far_block, to_core(far_block)))
    merged = match(held, far_keys, cap, sums)
    returned = [to_chip(m, j) for j, m in enumerate(merged)]
    places = place(owners, owner, count, cap)
    return unpack(places, returned, [to_core(m) for m in returned], cap)


def solution(mesh):
    own, help_ = mesh.shape["own"], mesh.shape["help"]
    near = 4
    split = Mesh(
        mesh.devices.reshape(2, own // 4, 2, near, help_ // near),
        ("z_hi", "z_lo", "core", "near", "far"),
    )
    where = ("z_hi", "z_lo", "core", "near", "far")
    return jax.shard_map(
        shards,
        mesh=split,
        in_specs=(P(where, None), P(where, None), P(where), P(where)),
        out_specs=P(where, None),
        check_vma=False,
    )
```

time: 118 us -> 60 us (0.51)
  blocking collectives: 37.8 us -> 0 us
  starting transfers between devices: 4.61 us -> 28.1 us
  matrix products: 17.9 us -> 0 us
  waiting for transfers between devices: 30.4 us -> 15.2 us
  between operations: 13.5 us -> 0.18 us
  Pallas kernels: 0 us -> 13.1 us
  other arithmetic: 8.15 us -> 0.01 us
  local copies, waits for them, and re-layouts: 5.24 us -> 3.16 us
    all_to_all x2 -> x0, blocking collectives: 29.5 us -> none  [the longest x1 21.6 us: shards(): lax.all_to_all(outbox.reshape(owners, capacity, width), 'own', split_axis...]
    ppermute x0 -> x27, starting transfers between devices: none -> 28.1 us  [the longest x12 22.1 us: to_chip(): return lax.ppermute(x, ('z_lo', 'core', 'near'), pairs)]
    dot_general x2 -> x0, matrix products: 17.9 us -> none  [the longest x1 9.72 us: pair_weights(): lax.dot_general(query_rows, key_rows, (((1,), (1,)), ((), ())), preferred...]
    all_to_all x1 -> x0, waiting for transfers between devices: 15.4 us -> none  [shards(): lax.all_to_all(merged, 'own', split_axis=0, concat_axis=0, tiled=True)]
    ppermute x0 -> x27, waiting for transfers between devices: none -> 15.2 us  [the longest x12 8.67 us: to_chip(): return lax.ppermute(x, ('z_lo', 'core', 'near'), pairs)]
    all_gather x1 -> x0, waiting for transfers between devices: 15 us -> none  [shards(): lax.all_gather(held_rows, 'help', axis=0, tiled=True)]
    pallas_call x0 -> x7, Pallas kernels: none -> 13.1 us  [the longest x2 7.48 us: match(): pl.pallas_call(functools.partial(match_kernel, count, cap, sums is not No...]
    all_gather x1 -> x0, blocking collectives: 8.34 us -> none  [shards(): lax.all_gather(held_codes, 'help', axis=0, tiled=True)]
  transfers between devices with their start and end apart: 2 -> 27, of which waited for: 2 -> 10; matrix products, arithmetic and copies ran while one was open for 3% -> 0% of each run, Pallas kernels for 0% -> 13%
where the time goes in v1:
time: 60 us; the launch traced here: 59.7 us
  starting transfers between devices  28.1 us (47%)
  waiting for transfers between devices  15.2 us (25%)
  Pallas kernels  13.1 us (22%)
  local copies, waits for them, and re-layouts  3.16 us (5%)
    ppermute x12, starting transfers between devices, to_chip(): return lax.ppermute(x, ('z_lo', 'core', 'near'), pairs)  22.1 us
    ppermute x12, waiting for transfers between devices, to_chip(): return lax.ppermute(x, ('z_lo', 'core', 'near'), pairs)  8.67 us
    pallas_call x2, Pallas kernels, match(): pl.pallas_call(functools.partial(match_kernel, count, cap, sums is not No...  7.48 us
    ppermute x1, waiting for transfers between devices, to_half(): return lax.ppermute(x, 'z_hi', SWAP)  6.49 us
    ppermute x1, starting transfers between devices, to_half(): return lax.ppermute(x, 'z_hi', SWAP)  3.66 us
    unnamed x13, local copies, waits for them, and re-layouts  3.16 us
    pallas_call x2, Pallas kernels, pack(): pl.pallas_call(functools.partial(pack_kernel, count, cap), in_specs=[pl.B...  3.06 us
    ppermute x14, starting transfers between devices, to_core(): return lax.ppermute(x, 'core', SWAP)  2.41 us
  transfers between devices with their start and end apart: 27, of which 10 were waited for; matrix products, arithmetic and copies ran while one was open for 0% of the time, Pallas kernels for 13%

profile of v1, /device:TPU:0, one launch (start us, length us, event | category | flops | bytes accessed | tf_op | source)
XLA Modules:
  0.0 59.7 jit_solution(12937629295934467091)
XLA Ops:
  0.7 0.9 %copy-done = bf16[512,256]{1,0:T(8,128)(2,1)S(1)} copy-done((bf16[512,256]{1,0:T(8,128)(2,1)S(1)}, bf16[512,256]{1,0:T(8,128)(2,1)}, u32[]{:S(2)}) %copy-start) | copy-done | bytes 262168
  3.0 3.7 %collective-permute-start.9 = (bf16[520,256]{1,0:T(8,128)(2,1)S(1)}, bf16[520,256]{1,0:T(8,128)(2,1)S(1)}, u32[]{:S(2)}, u32[]{:S(2)}) collective-permute-start(bf16[520,256]{1,0:T(8,128)(2,1)S(1)} %shard_map.56.refs_0_), channel_id=1, source_target_pairs={{0,16},{16,0},{1,17},{17,1},{2,18},{18,2},{3,19},{19,3},{4,20},{20... | collective-permute-start | bytes 798728 | tf_op jit(solution)/shard_map/ppermute | solution.py:249
  7.4 1.5 %shard_map.57 = (bf16[2,136,256]{2,1,0:T(8,128)(2,1)S(1)}, bf16[2,136,256]{2,1,0:T(8,128)(2,1)S(1)}, bf16[2,136,256]{2,1,0:T(8,128)(2,1)S(1)}, bf16[2,136,256]{2,1,0:T(8,128)(2,1)S(1)}) custom-call(s32[2,4]{1,0:T(2,128)S(1)} %select_xor_fusion.owners_ref, bf16[520,256]{1,0:T(8,128)(2,1)S(1)} %shard_map.56.refs_0_, ...), custom_call_target="tpu_custom_call" | custom-call | tf_op jit(solution)/shard_map/pallas_call | solution.py:91
  8.9 3.5 %collective-permute-start.1 = (bf16[2,136,256]{2,1,0:T(8,128)(2,1)S(1)}, bf16[2,136,256]{2,1,0:T(8,128)(2,1)S(1)}, u32[]{:S(2)}, u32[]{:S(2)}) collective-permute-start(bf16[2,136,256]{2,1,0:T(8,128)(2,1)S(1)} %get-tuple-element.19), channel_id=1, source_target_pairs={{0,11},{1,10},{2,9},{3,8},{8,3},{9,2},{10,1},{11,0},{4,7},{5,6},{6... | collective-permute-start | bytes 417800 | tf_op jit(solution)/shard_map/ppermute | solution.py:258
  13.0 6.5 %collective-permute-done.9.refs_0_ = bf16[520,256]{1,0:T(8,128)(2,1)S(1)} collective-permute-done((bf16[520,256]{1,0:T(8,128)(2,1)S(1)}, bf16[520,256]{1,0:T(8,128)(2,1)S(1)}, u32[]{:S(2)}, u32[]{:S(2)}) %collective-permute-start.9) | collective-permute-done | bytes 266272 | tf_op jit(solution)/shard_map/ppermute | solution.py:249
  19.5 1.6 %collective-permute-start.3 = (bf16[2,136,256]{2,1,0:T(8,128)(2,1)S(1)}, bf16[2,136,256]{2,1,0:T(8,128)(2,1)S(1)}, u32[]{:S(2)}, u32[]{:S(2)}) collective-permute-start(bf16[2,136,256]{2,1,0:T(8,128)(2,1)S(1)} %get-tuple-element.21), channel_id=1, source_target_pairs={{0,2},{1,3},{2,0},{3,1},{8,10},{9,11},{10,8},{11,9},{4,14},{5,15},... | collective-permute-start | bytes 417800 | tf_op jit(solution)/shard_map/ppermute | solution.py:258
  21.1 2.6 %collective-permute-start.4 = (bf16[2,136,256]{2,1,0:T(8,128)(2,1)S(1)}, bf16[2,136,256]{2,1,0:T(8,128)(2,1)S(1)}, u32[]{:S(2)}, u32[]{:S(2)}) collective-permute-start(bf16[2,136,256]{2,1,0:T(8,128)(2,1)S(1)} %get-tuple-element.22), channel_id=1, source_target_pairs={{0,8},{1,9},{2,10},{3,11},{8,0},{9,1},{10,2},{11,3},{4,4},{5,5},{6... | collective-permute-start | bytes 417800 | tf_op jit(solution)/shard_map/ppermute | solution.py:258
  24.2 1.8 %collective-permute-done.3.refs_2_.refs_6_ = bf16[2,136,256]{2,1,0:T(8,128)(2,1)S(1)} collective-permute-done((bf16[2,136,256]{2,1,0:T(8,128)(2,1)S(1)}, bf16[2,136,256]{2,1,0:T(8,128)(2,1)S(1)}, u32[]{:S(2)}, u32[]{:S(2)}) %collective-permute-start.3) | collective-permute-done | bytes 139296 | tf_op jit(solution)/shard_map/ppermute | solution.py:258
  26.0 1.5 %shard_map.59 = (bf16[2,136,256]{2,1,0:T(8,128)(2,1)S(1)}, bf16[2,136,256]{2,1,0:T(8,128)(2,1)S(1)}, bf16[2,136,256]{2,1,0:T(8,128)(2,1)S(1)}, bf16[2,136,256]{2,1,0:T(8,128)(2,1)S(1)}) custom-call(s32[2,4]{1,0:T(2,128)S(1)} %select_xor_fusion.owners_ref, bf16[520,256]{1,0:T(8,128)(2,1)S(1)} %collective-permute-done.9.refs_0_, ...), custom_call_target="tpu_custom_call" | custom-call | tf_op jit(solution)/shard_map/pallas_call | solution.py:91
  27.6 2.6 %collective-permute-start.11 = (bf16[2,136,256]{2,1,0:T(8,128)(2,1)S(1)}, bf16[2,136,256]{2,1,0:T(8,128)(2,1)S(1)}, u32[]{:S(2)}, u32[]{:S(2)}) collective-permute-start(bf16[2,136,256]{2,1,0:T(8,128)(2,1)S(1)} %get-tuple-element.25), channel_id=1, source_target_pairs={{0,11},{1,10},{2,9},{3,8},{8,3},{9,2},{10,1},{11,0},{4,7},{5,6},{6... | collective-permute-start | bytes 417800 | tf_op jit(solution)/shard_map/ppermute | solution.py:258
  31.3 3.2 %collective-permute-start.14 = (bf16[2,136,256]{2,1,0:T(8,128)(2,1)S(1)}, bf16[2,136,256]{2,1,0:T(8,128)(2,1)S(1)}, u32[]{:S(2)}, u32[]{:S(2)}) collective-permute-start(bf16[2,136,256]{2,1,0:T(8,128)(2,1)S(1)} %get-tuple-element.28), channel_id=1, source_target_pairs={{0,8},{1,9},{2,10},{3,11},{8,0},{9,1},{10,2},{11,3},{4,4},{5,5},{6... | collective-permute-start | bytes 417800 | tf_op jit(solution)/shard_map/ppermute | solution.py:258
  34.6 0.7 %collective-permute-done.11.refs_6_ = bf16[2,136,256]{2,1,0:T(8,128)(2,1)S(1)} collective-permute-done((bf16[2,136,256]{2,1,0:T(8,128)(2,1)S(1)}, bf16[2,136,256]{2,1,0:T(8,128)(2,1)S(1)}, u32[]{:S(2)}, u32[]{:S(2)}) %collective-permute-start.11) | collective-permute-done | bytes 139296 | tf_op jit(solution)/shard_map/ppermute | solution.py:258
  35.3 0.8 %collective-permute-start.15 = (bf16[2,136,256]{2,1,0:T(8,128)(2,1)S(1)}, bf16[2,136,256]{2,1,0:T(8,128)(2,1)S(1)}, u32[]{:S(2)}, u32[]{:S(2)}) collective-permute-start(bf16[2,136,256]{2,1,0:T(8,128)(2,1)S(1)} %collective-permute-done.11.refs_6_), channel_id=1, source_target_pairs={{0,4},{4,0},{1,5},{5,1},{2,6},{6,2},{3,7},{7,3},{8,12},{12,8},{9,1... | collective-permute-start | bytes 417800 | tf_op jit(solution)/shard_map/ppermute | solution.py:246
  36.0 1.7 %collective-permute-done.12.refs_7_ = bf16[2,136,256]{2,1,0:T(8,128)(2,1)S(1)} collective-permute-done((bf16[2,136,256]{2,1,0:T(8,128)(2,1)S(1)}, bf16[2,136,256]{2,1,0:T(8,128)(2,1)S(1)}, u32[]{:S(2)}, u32[]{:S(2)}) %collective-permute-start.12) | collective-permute-done | bytes 139296 | tf_op jit(solution)/shard_map/ppermute | solution.py:258
  38.2 0.7 %collective-permute-done.14.refs_9_ = bf16[2,136,256]{2,1,0:T(8,128)(2,1)S(1)} collective-permute-done((bf16[2,136,256]{2,1,0:T(8,128)(2,1)S(1)}, bf16[2,136,256]{2,1,0:T(8,128)(2,1)S(1)}, u32[]{:S(2)}, u32[]{:S(2)}) %collective-permute-start.14) | collective-permute-done | bytes 139296 | tf_op jit(solution)/shard_map/ppermute | solution.py:258
  39.0 3.8 %shard_map.58 = (f32[1024,256]{1,0:T(8,128)S(1)}, f32[1024,1]{1,0:T(8,128)S(1)}) custom-call(bf16[2,136,256]{2,1,0:T(8,128)(2,1)S(1)} %collective-permute-done.1.refs_0_.refs_4_, bf16[2,136,256]{2,1,0:T(8,128)(2,1)S(1)} %collective-permute-done.2.refs_1_.refs_5_, bf16[2,136,256]{2,1,0:T(8,128)(2,1)S(1)} %collective-permute-done.3.refs_2_.refs_6_, ...), custom_call_target="tpu_custom_call" | custom-call | tf_op jit(solution)/shard_map/pallas_call | solution.py:201
  42.8 3.6 %shard_map.60 = (bf16[2,128,256]{2,1,0:T(8,128)(2,1)S(1)}, bf16[2,128,256]{2,1,0:T(8,128)(2,1)S(1)}, bf16[2,128,256]{2,1,0:T(8,128)(2,1)S(1)}, bf16[2,128,256]{2,1,0:T(8,128)(2,1)S(1)}) custom-call(bf16[2,136,256]{2,1,0:T(8,128)(2,1)S(1)} %collective-permute-done.1.refs_0_.refs_4_, bf16[2,136,256]{2,1,0:T(8,128)(2,1)S(1)} %collective-permute-done.2.refs_1_.refs_5_, ...), custom_call_target="tpu_custom_call" | custom-call | tf_op jit(solution)/shard_map/pallas_call | solution.py:201
  46.5 2.6 %collective-permute-start.19 = (bf16[2,128,256]{2,1,0:T(8,128)(2,1)S(1)}, bf16[2,128,256]{2,1,0:T(8,128)(2,1)S(1)}, u32[]{:S(2)}, u32[]{:S(2)}) collective-permute-start(bf16[2,128,256]{2,1,0:T(8,128)(2,1)S(1)} %get-tuple-element.29), channel_id=1, source_target_pairs={{0,11},{1,10},{2,9},{3,8},{8,3},{9,2},{10,1},{11,0},{4,7},{5,6},{6... | collective-permute-start | bytes 393224 | tf_op jit(solution)/shard_map/ppermute | solution.py:258
  50.2 3.2 %collective-permute-start.22 = (bf16[2,128,256]{2,1,0:T(8,128)(2,1)S(1)}, bf16[2,128,256]{2,1,0:T(8,128)(2,1)S(1)}, u32[]{:S(2)}, u32[]{:S(2)}) collective-permute-start(bf16[2,128,256]{2,1,0:T(8,128)(2,1)S(1)} %get-tuple-element.32), channel_id=1, source_target_pairs={{0,8},{1,9},{2,10},{3,11},{8,0},{9,1},{10,2},{11,3},{4,4},{5,5},{6... | collective-permute-start | bytes 393224 | tf_op jit(solution)/shard_map/ppermute | solution.py:258
  53.4 1.2 %collective-permute-done.19.refs_0_ = bf16[2,128,256]{2,1,0:T(8,128)(2,1)S(1)} collective-permute-done((bf16[2,128,256]{2,1,0:T(8,128)(2,1)S(1)}, bf16[2,128,256]{2,1,0:T(8,128)(2,1)S(1)}, u32[]{:S(2)}, u32[]{:S(2)}) %collective-permute-start.19) | collective-permute-done | bytes 131104 | tf_op jit(solution)/shard_map/ppermute | solution.py:258
  54.7 0.9 %collective-permute-done.20.refs_1_ = bf16[2,128,256]{2,1,0:T(8,128)(2,1)S(1)} collective-permute-done((bf16[2,128,256]{2,1,0:T(8,128)(2,1)S(1)}, bf16[2,128,256]{2,1,0:T(8,128)(2,1)S(1)}, u32[]{:S(2)}, u32[]{:S(2)}) %collective-permute-start.20) | collective-permute-done | bytes 131104 | tf_op jit(solution)/shard_map/ppermute | solution.py:258
  55.5 1.1 %collective-permute-done.21.refs_2_ = bf16[2,128,256]{2,1,0:T(8,128)(2,1)S(1)} collective-permute-done((bf16[2,128,256]{2,1,0:T(8,128)(2,1)S(1)}, bf16[2,128,256]{2,1,0:T(8,128)(2,1)S(1)}, u32[]{:S(2)}, u32[]{:S(2)}) %collective-permute-start.21) | collective-permute-done | bytes 131104 | tf_op jit(solution)/shard_map/ppermute | solution.py:258
  57.3 1.1 %shard_map.55.place_ref = s32[512,1]{1,0:T(8,128)S(1)} custom-call(s32[2,4]{1,0:T(2,128)S(1)} %select_xor_fusion.owners_ref, s32[512,1]{1,0:T(8,128)S(1)} %copy.6.owner_ref), custom_call_target="tpu_custom_call" | custom-call | tf_op jit(solution)/shard_map/pallas_call | solution.py:121
  58.4 1.3 %shard_map.61 = bf16[512,256]{1,0:T(8,128)(2,1)} custom-call(s32[512,1]{1,0:T(8,128)S(1)} %shard_map.55.place_ref, bf16[2,128,256]{2,1,0:T(8,128)(2,1)S(1)} %collective-permute-done.19.refs_0_, bf16[2,128,256]{2,1,0:T(8,128)(2,1)S(1)} %collective-permute-done.20.refs_1_, bf16[2,128,256]{2,1,0:T(8,128)(2,1)S(1)} %collective-permute-done.21.refs_2_, ...), custom_call_target="tpu_custom_call" | custom-call | tf_op jit(solution)/shard_map/pallas_call | solution.py:223
  (51 shorter events, 7.4 us)
Async XLA Ops:
  2.5 4.9 %collective-permute-start = (bf16[520,256]{1,0:T(8,128)(2,1)S(1)}, bf16[520,256]{1,0:T(8,128)(2,1)S(1)}, u32[]{:S(2)}, u32[]{:S(2)}) collective-permute-start(bf16[520,256]{1,0:T(8,128)(2,1)S(1)} %shard_map.56.refs_0_), channel_id=1, source_target_pairs={{0,4},{4,0},{1,5},{5,1},{2,6},{6,2},{3,7},{7,3},{8,12},{12,8},{9,1... | collective-permute-start | bytes 798728 | tf_op jit(solution)/shard_map/ppermute | solution.py:246
  3.0 16.5 %collective-permute-start.9 = (bf16[520,256]{1,0:T(8,128)(2,1)S(1)}, bf16[520,256]{1,0:T(8,128)(2,1)S(1)}, u32[]{:S(2)}, u32[]{:S(2)}) collective-permute-start(bf16[520,256]{1,0:T(8,128)(2,1)S(1)} %shard_map.56.refs_0_), channel_id=1, source_target_pairs={{0,16},{16,0},{1,17},{17,1},{2,18},{18,2},{3,19},{19,3},{4,20},{20... | collective-permute-start | bytes 798728 | tf_op jit(solution)/shard_map/ppermute | solution.py:249
  8.9 14.7 %collective-permute-start.1 = (bf16[2,136,256]{2,1,0:T(8,128)(2,1)S(1)}, bf16[2,136,256]{2,1,0:T(8,128)(2,1)S(1)}, u32[]{:S(2)}, u32[]{:S(2)}) collective-permute-start(bf16[2,136,256]{2,1,0:T(8,128)(2,1)S(1)} %get-tuple-element.19), channel_id=1, source_target_pairs={{0,11},{1,10},{2,9},{3,8},{8,3},{9,2},{10,1},{11,0},{4,7},{5,6},{6... | collective-permute-start | bytes 417800 | tf_op jit(solution)/shard_map/ppermute | solution.py:258
  12.4 11.3 %collective-permute-start.2 = (bf16[2,136,256]{2,1,0:T(8,128)(2,1)S(1)}, bf16[2,136,256]{2,1,0:T(8,128)(2,1)S(1)}, u32[]{:S(2)}, u32[]{:S(2)}) collective-permute-start(bf16[2,136,256]{2,1,0:T(8,128)(2,1)S(1)} %get-tuple-element.20), channel_id=1, source_target_pairs={{0,1},{1,0},{2,3},{3,2},{8,9},{9,8},{10,11},{11,10},{4,13},{5,12},... | collective-permute-start | bytes 417800 | tf_op jit(solution)/shard_map/ppermute | solution.py:258
  19.5 6.6 %collective-permute-start.10 = (bf16[520,256]{1,0:T(8,128)(2,1)S(1)}, bf16[520,256]{1,0:T(8,128)(2,1)S(1)}, u32[]{:S(2)}, u32[]{:S(2)}) collective-permute-start(bf16[520,256]{1,0:T(8,128)(2,1)S(1)} %collective-permute-done.9.refs_0_), channel_id=1, source_target_pairs={{0,4},{4,0},{1,5},{5,1},{2,6},{6,2},{3,7},{7,3},{8,12},{12,8},{9,1... | collective-permute-start | bytes 798728 | tf_op jit(solution)/shard_map/ppermute | solution.py:246
  19.5 6.5 %collective-permute-start.3 = (bf16[2,136,256]{2,1,0:T(8,128)(2,1)S(1)}, bf16[2,136,256]{2,1,0:T(8,128)(2,1)S(1)}, u32[]{:S(2)}, u32[]{:S(2)}) collective-permute-start(bf16[2,136,256]{2,1,0:T(8,128)(2,1)S(1)} %get-tuple-element.21), channel_id=1, source_target_pairs={{0,2},{1,3},{2,0},{3,1},{8,10},{9,11},{10,8},{11,9},{4,14},{5,15},... | collective-permute-start | bytes 417800 | tf_op jit(solution)/shard_map/ppermute | solution.py:258
  21.1 9.2 %collective-permute-start.4 = (bf16[2,136,256]{2,1,0:T(8,128)(2,1)S(1)}, bf16[2,136,256]{2,1,0:T(8,128)(2,1)S(1)}, u32[]{:S(2)}, u32[]{:S(2)}) collective-permute-start(bf16[2,136,256]{2,1,0:T(8,128)(2,1)S(1)} %get-tuple-element.22), channel_id=1, source_target_pairs={{0,8},{1,9},{2,10},{3,11},{8,0},{9,1},{10,2},{11,3},{4,4},{5,5},{6... | collective-permute-start | bytes 417800 | tf_op jit(solution)/shard_map/ppermute | solution.py:258
  23.7 7.1 %collective-permute-start.5 = (bf16[2,136,256]{2,1,0:T(8,128)(2,1)S(1)}, bf16[2,136,256]{2,1,0:T(8,128)(2,1)S(1)}, u32[]{:S(2)}, u32[]{:S(2)}) collective-permute-start(bf16[2,136,256]{2,1,0:T(8,128)(2,1)S(1)} %collective-permute-done.1.refs_0_.refs_4_), channel_id=1, source_target_pairs={{0,4},{4,0},{1,5},{5,1},{2,6},{6,2},{3,7},{7,3},{8,12},{12,8},{9,1... | collective-permute-start | bytes 417800 | tf_op jit(solution)/shard_map/ppermute | solution.py:246
  23.7 7.6 %collective-permute-start.6 = (bf16[2,136,256]{2,1,0:T(8,128)(2,1)S(1)}, bf16[2,136,256]{2,1,0:T(8,128)(2,1)S(1)}, u32[]{:S(2)}, u32[]{:S(2)}) collective-permute-start(bf16[2,136,256]{2,1,0:T(8,128)(2,1)S(1)} %collective-permute-done.2.refs_1_.refs_5_), channel_id=1, source_target_pairs={{0,4},{4,0},{1,5},{5,1},{2,6},{6,2},{3,7},{7,3},{8,12},{12,8},{9,1... | collective-permute-start | bytes 417800 | tf_op jit(solution)/shard_map/ppermute | solution.py:246
  26.0 8.5 %collective-permute-start.7 = (bf16[2,136,256]{2,1,0:T(8,128)(2,1)S(1)}, bf16[2,136,256]{2,1,0:T(8,128)(2,1)S(1)}, u32[]{:S(2)}, u32[]{:S(2)}) collective-permute-start(bf16[2,136,256]{2,1,0:T(8,128)(2,1)S(1)} %collective-permute-done.3.refs_2_.refs_6_), channel_id=1, source_target_pairs={{0,4},{4,0},{1,5},{5,1},{2,6},{6,2},{3,7},{7,3},{8,12},{12,8},{9,1... | collective-permute-start | bytes 417800 | tf_op jit(solution)/shard_map/ppermute | solution.py:246
  27.6 7.7 %collective-permute-start.11 = (bf16[2,136,256]{2,1,0:T(8,128)(2,1)S(1)}, bf16[2,136,256]{2,1,0:T(8,128)(2,1)S(1)}, u32[]{:S(2)}, u32[]{:S(2)}) collective-permute-start(bf16[2,136,256]{2,1,0:T(8,128)(2,1)S(1)} %get-tuple-element.25), channel_id=1, source_target_pairs={{0,11},{1,10},{2,9},{3,8},{8,3},{9,2},{10,1},{11,0},{4,7},{5,6},{6... | collective-permute-start | bytes 417800 | tf_op jit(solution)/shard_map/ppermute | solution.py:258
  30.2 7.5 %collective-permute-start.12 = (bf16[2,136,256]{2,1,0:T(8,128)(2,1)S(1)}, bf16[2,136,256]{2,1,0:T(8,128)(2,1)S(1)}, u32[]{:S(2)}, u32[]{:S(2)}) collective-permute-start(bf16[2,136,256]{2,1,0:T(8,128)(2,1)S(1)} %get-tuple-element.26), channel_id=1, source_target_pairs={{0,1},{1,0},{2,3},{3,2},{8,9},{9,8},{10,11},{11,10},{4,13},{5,12},... | collective-permute-start | bytes 417800 | tf_op jit(solution)/shard_map/ppermute | solution.py:258
  30.8 7.0 %collective-permute-start.13 = (bf16[2,136,256]{2,1,0:T(8,128)(2,1)S(1)}, bf16[2,136,256]{2,1,0:T(8,128)(2,1)S(1)}, u32[]{:S(2)}, u32[]{:S(2)}) collective-permute-start(bf16[2,136,256]{2,1,0:T(8,128)(2,1)S(1)} %get-tuple-element.27), channel_id=1, source_target_pairs={{0,2},{1,3},{2,0},{3,1},{8,10},{9,11},{10,8},{11,9},{4,14},{5,15},... | collective-permute-start | bytes 417800 | tf_op jit(solution)/shard_map/ppermute | solution.py:258
  31.3 7.6 %collective-permute-start.14 = (bf16[2,136,256]{2,1,0:T(8,128)(2,1)S(1)}, bf16[2,136,256]{2,1,0:T(8,128)(2,1)S(1)}, u32[]{:S(2)}, u32[]{:S(2)}) collective-permute-start(bf16[2,136,256]{2,1,0:T(8,128)(2,1)S(1)} %get-tuple-element.28), channel_id=1, source_target_pairs={{0,8},{1,9},{2,10},{3,11},{8,0},{9,1},{10,2},{11,3},{4,4},{5,5},{6... | collective-permute-start | bytes 417800 | tf_op jit(solution)/shard_map/ppermute | solution.py:258
  34.5 4.4 %collective-permute-start.8 = (bf16[2,136,256]{2,1,0:T(8,128)(2,1)S(1)}, bf16[2,136,256]{2,1,0:T(8,128)(2,1)S(1)}, u32[]{:S(2)}, u32[]{:S(2)}) collective-permute-start(bf16[2,136,256]{2,1,0:T(8,128)(2,1)S(1)} %collective-permute-done.4.refs_3_.refs_7_), channel_id=1, source_target_pairs={{0,4},{4,0},{1,5},{5,1},{2,6},{6,2},{3,7},{7,3},{8,12},{12,8},{9,1... | collective-permute-start | bytes 417800 | tf_op jit(solution)/shard_map/ppermute | solution.py:246
  35.3 7.5 %collective-permute-start.15 = (bf16[2,136,256]{2,1,0:T(8,128)(2,1)S(1)}, bf16[2,136,256]{2,1,0:T(8,128)(2,1)S(1)}, u32[]{:S(2)}, u32[]{:S(2)}) collective-permute-start(bf16[2,136,256]{2,1,0:T(8,128)(2,1)S(1)} %collective-permute-done.11.refs_6_), channel_id=1, source_target_pairs={{0,4},{4,0},{1,5},{5,1},{2,6},{6,2},{3,7},{7,3},{8,12},{12,8},{9,1... | collective-permute-start | bytes 417800 | tf_op jit(solution)/shard_map/ppermute | solution.py:246
  37.7 5.1 %collective-permute-start.16 = (bf16[2,136,256]{2,1,0:T(8,128)(2,1)S(1)}, bf16[2,136,256]{2,1,0:T(8,128)(2,1)S(1)}, u32[]{:S(2)}, u32[]{:S(2)}) collective-permute-start(bf16[2,136,256]{2,1,0:T(8,128)(2,1)S(1)} %collective-permute-done.12.refs_7_), channel_id=1, source_target_pairs={{0,4},{4,0},{1,5},{5,1},{2,6},{6,2},{3,7},{7,3},{8,12},{12,8},{9,1... | collective-permute-start | bytes 417800 | tf_op jit(solution)/shard_map/ppermute | solution.py:246
  37.8 5.0 %collective-permute-start.17 = (bf16[2,136,256]{2,1,0:T(8,128)(2,1)S(1)}, bf16[2,136,256]{2,1,0:T(8,128)(2,1)S(1)}, u32[]{:S(2)}, u32[]{:S(2)}) collective-permute-start(bf16[2,136,256]{2,1,0:T(8,128)(2,1)S(1)} %collective-permute-done.13.refs_8_), channel_id=1, source_target_pairs={{0,4},{4,0},{1,5},{5,1},{2,6},{6,2},{3,7},{7,3},{8,12},{12,8},{9,1... | collective-permute-start | bytes 417800 | tf_op jit(solution)/shard_map/ppermute | solution.py:246
  38.9 3.9 %collective-permute-start.18 = (bf16[2,136,256]{2,1,0:T(8,128)(2,1)S(1)}, bf16[2,136,256]{2,1,0:T(8,128)(2,1)S(1)}, u32[]{:S(2)}, u32[]{:S(2)}) collective-permute-start(bf16[2,136,256]{2,1,0:T(8,128)(2,1)S(1)} %collective-permute-done.14.refs_9_), channel_id=1, source_target_pairs={{0,4},{4,0},{1,5},{5,1},{2,6},{6,2},{3,7},{7,3},{8,12},{12,8},{9,1... | collective-permute-start | bytes 417800 | tf_op jit(solution)/shard_map/ppermute | solution.py:246
  46.5 8.2 %collective-permute-start.19 = (bf16[2,128,256]{2,1,0:T(8,128)(2,1)S(1)}, bf16[2,128,256]{2,1,0:T(8,128)(2,1)S(1)}, u32[]{:S(2)}, u32[]{:S(2)}) collective-permute-start(bf16[2,128,256]{2,1,0:T(8,128)(2,1)S(1)} %get-tuple-element.29), channel_id=1, source_target_pairs={{0,11},{1,10},{2,9},{3,8},{8,3},{9,2},{10,1},{11,0},{4,7},{5,6},{6... | collective-permute-start | bytes 393224 | tf_op jit(solution)/shard_map/ppermute | solution.py:258
  49.1 6.4 %collective-permute-start.20 = (bf16[2,128,256]{2,1,0:T(8,128)(2,1)S(1)}, bf16[2,128,256]{2,1,0:T(8,128)(2,1)S(1)}, u32[]{:S(2)}, u32[]{:S(2)}) collective-permute-start(bf16[2,128,256]{2,1,0:T(8,128)(2,1)S(1)} %get-tuple-element.30), channel_id=1, source_target_pairs={{0,1},{1,0},{2,3},{3,2},{8,9},{9,8},{10,11},{11,10},{4,13},{5,12},... | collective-permute-start | bytes 393224 | tf_op jit(solution)/shard_map/ppermute | solution.py:258
  49.6 7.0 %collective-permute-start.21 = (bf16[2,128,256]{2,1,0:T(8,128)(2,1)S(1)}, bf16[2,128,256]{2,1,0:T(8,128)(2,1)S(1)}, u32[]{:S(2)}, u32[]{:S(2)}) collective-permute-start(bf16[2,128,256]{2,1,0:T(8,128)(2,1)S(1)} %get-tuple-element.31), channel_id=1, source_target_pairs={{0,2},{1,3},{2,0},{3,1},{8,10},{9,11},{10,8},{11,9},{4,14},{5,15},... | collective-permute-start | bytes 393224 | tf_op jit(solution)/shard_map/ppermute | solution.py:258
  50.2 6.8 %collective-permute-start.22 = (bf16[2,128,256]{2,1,0:T(8,128)(2,1)S(1)}, bf16[2,128,256]{2,1,0:T(8,128)(2,1)S(1)}, u32[]{:S(2)}, u32[]{:S(2)}) collective-permute-start(bf16[2,128,256]{2,1,0:T(8,128)(2,1)S(1)} %get-tuple-element.32), channel_id=1, source_target_pairs={{0,8},{1,9},{2,10},{3,11},{8,0},{9,1},{10,2},{11,3},{4,4},{5,5},{6... | collective-permute-start | bytes 393224 | tf_op jit(solution)/shard_map/ppermute | solution.py:258
  54.7 3.7 %collective-permute-start.23 = (bf16[2,128,256]{2,1,0:T(8,128)(2,1)S(1)}, bf16[2,128,256]{2,1,0:T(8,128)(2,1)S(1)}, u32[]{:S(2)}, u32[]{:S(2)}) collective-permute-start(bf16[2,128,256]{2,1,0:T(8,128)(2,1)S(1)} %collective-permute-done.19.refs_0_), channel_id=1, source_target_pairs={{0,4},{4,0},{1,5},{5,1},{2,6},{6,2},{3,7},{7,3},{8,12},{12,8},{9,1... | collective-permute-start | bytes 393224 | tf_op jit(solution)/shard_map/ppermute | solution.py:246
  (9 other events, 10.3 us)

commit v2 on v1

--- a/solution.py
+++ b/solution.py
@@ -19,13 +19,21 @@
 VMEM_LIMIT = 48 * 2**20
 
 
-def selections(full_codes, owner_of, count, cap):
+def owners_here(flips):
+    core = lax.axis_index("core")
+    spot = lax.axis_index("z_lo") * lax.axis_size("near") + lax.axis_index("near")
+    mine = [spot ^ jnp.where(core == 0, a, b) for a, b in zip(*flips)]
+    return mine, [spot ^ jnp.where(core == 0, b, a) for a, b in zip(*flips)]
+
+
+def selections(full_codes, owners, cap):
     rows = full_codes.shape[1]
+    count = len(owners)
     lines = max(8, count)
     line = lax.broadcasted_iota(jnp.int32, (lines, rows), 0)
     wanted = jnp.full((lines, rows), -1, jnp.int32)
     for j in range(count):
-        wanted = jnp.where(line == j, owner_of(j), wanted)
+        wanted = jnp.where(line == j, owners[j], wanted)
     named = wanted == jnp.broadcast_to(full_codes // CODES, (lines, rows))
     before = lax.broadcasted_iota(jnp.int32, (rows, rows), 0)
     after = lax.broadcasted_iota(jnp.int32, (rows, rows), 1)
@@ -43,12 +51,19 @@
     ]
 
 
-def scale_kernel(rows_ref, owner_ref, subkey_ref, source_ref, out_ref):
+def scale_kernel(rows_hbm, owner_hbm, subkey_hbm, source_hbm, out_ref, rows_ref, ids_ref, sems):
     rows, width = rows_ref.shape
+    copies = [pltpu.make_async_copy(rows_hbm, rows_ref, sems.at[0])]
+    for i, hbm in enumerate((owner_hbm, subkey_hbm, source_hbm)):
+        copies.append(pltpu.make_async_copy(hbm, ids_ref.at[i], sems.at[i + 1]))
+    for copy in copies:
+        copy.start()
+    for copy in copies:
+        copy.wait()
     values = rows_ref[...].astype(jnp.float32)
     inverse = lax.rsqrt(jnp.mean(values * values, axis=1, keepdims=True) + EPSILON)
     out_ref[:rows, :] = (values * inverse).astype(jnp.bfloat16)
-    codes = (owner_ref[...] * SUBKEYS + subkey_ref[...]) * SOURCES + source_ref[...]
+    codes = (ids_ref[0] * SUBKEYS + ids_ref[1]) * SOURCES + ids_ref[2]
     line = lax.broadcasted_iota(jnp.int32, (PAD, width), 0)
     lines = jnp.zeros((PAD, width), jnp.int32)
     for k in range(rows // width):
@@ -60,13 +75,27 @@
     rows, width = records.shape
     return pl.pallas_call(
         scale_kernel,
+        in_specs=[pl.BlockSpec(memory_space=pltpu.HBM)] * 4,
+        out_specs=pl.BlockSpec(memory_space=pltpu.VMEM),
         out_shape=jax.ShapeDtypeStruct((rows + PAD, width), jnp.bfloat16),
-        compiler_params=pltpu.CompilerParams(vmem_limit_bytes=VMEM_LIMIT),
-    )(records, owner.reshape(1, rows), subkey.reshape(1, rows), source.reshape(1, rows))
-
-
-def pack_kernel(count, cap, owners_ref, *refs):
+        scratch_shapes=[
+            pltpu.VMEM((rows, width), jnp.bfloat16),
+            pltpu.VMEM((3, 1, rows), jnp.int32),
+            pltpu.SemaphoreType.DMA((4,)),
+        ],
+        compiler_params=pltpu.CompilerParams(vmem_limit_bytes=VMEM_LIMIT),
+    )(
+        *(
+            pltpu.with_memory_space_constraint(x, pltpu.HBM)
+            for x in (records, *(i.reshape(1, rows) for i in (owner, subkey, source)))
+        )
+    )
+
+
+def pack_kernel(flips, cap, *refs):
     blocks, messages = refs[:2], refs[2:]
+    count = len(messages)
+    owners, _ = owners_here(flips)
     for part in range(2):
         width = blocks[part].shape[1]
         rows = blocks[part].shape[0] - PAD
@@ -77,7 +106,7 @@
         ).astype(jnp.int32)
         codes = jnp.broadcast_to(full_codes % CODES + 1, (8, rows))
         codes = codes.astype(jnp.float32).astype(jnp.bfloat16)
-        picks = selections(full_codes, lambda j: owners_ref[0, j], count, cap)
+        picks = selections(full_codes, owners, cap)
         for j in range(count):
             picked = jnp.dot(picks[j], scaled, preferred_element_type=jnp.float32)
             messages[j][part, :cap, :] = picked.astype(jnp.bfloat16)
@@ -86,19 +115,19 @@
             messages[j][part, cap:, :cap] = line.astype(jnp.bfloat16)
 
 
-def pack(owners, blocks, count, cap):
+def pack(blocks, flips, cap):
+    count = len(flips[0])
     shape = jax.ShapeDtypeStruct((2, cap + PAD, blocks[0].shape[1]), jnp.bfloat16)
     return pl.pallas_call(
-        functools.partial(pack_kernel, count, cap),
-        in_specs=[pl.BlockSpec(memory_space=pltpu.SMEM)]
-        + [pl.BlockSpec(memory_space=pltpu.VMEM)] * 2,
+        functools.partial(pack_kernel, flips, cap),
+        in_specs=[pl.BlockSpec(memory_space=pltpu.VMEM)] * 2,
         out_specs=[pl.BlockSpec(memory_space=pltpu.VMEM)] * count,
         out_shape=[shape] * count,
         compiler_params=pltpu.CompilerParams(vmem_limit_bytes=VMEM_LIMIT),
-    )(owners, *blocks)
-
-
-def place_kernel(count, cap, owners_ref, owner_ref, out_ref):
+    )(*blocks)
+
+
+def place_kernel(flips, cap, owner_ref, out_ref):
     rows = owner_ref.shape[0]
     owner = owner_ref[...]
     lane = lax.broadcasted_iota(jnp.int32, (rows, 128), 1)
@@ -112,40 +141,38 @@
         preferred_element_type=jnp.float32,
     )
     rank = jnp.sum(jnp.where(named, rank, 0.0), axis=1, keepdims=True).astype(jnp.int32)
-    for i in range(2 * count):
-        rank = rank + jnp.where(owner == owners_ref[i // count, i % count], i * cap, 0)
+    mine, sibling = owners_here(flips)
+    for i, wanted in enumerate(mine + sibling):
+        rank = rank + jnp.where(owner == wanted, i * cap, 0)
     out_ref[...] = rank
 
 
-def place(owners, owner, count, cap):
-    return pl.pallas_call(
-        functools.partial(place_kernel, count, cap),
-        in_specs=[
-            pl.BlockSpec(memory_space=pltpu.SMEM),
-            pl.BlockSpec(memory_space=pltpu.VMEM),
-        ],
+def place(owner, flips, cap):
+    return pl.pallas_call(
+        functools.partial(place_kernel, flips, cap),
+        in_specs=[pl.BlockSpec(memory_space=pltpu.VMEM)],
         out_specs=pl.BlockSpec(memory_space=pltpu.VMEM),
         out_shape=jax.ShapeDtypeStruct(owner.shape, jnp.int32),
         compiler_params=pltpu.CompilerParams(vmem_limit_bytes=VMEM_LIMIT),
-    )(owners, owner)
+    )(owner)
 
 
 def code_line(ref, part, cap):
     return ref[part, cap : cap + 8, :cap].astype(jnp.float32)[0:1, :].astype(jnp.int32) - 1
 
 
-def match_kernel(queries, cap, last, *refs):
+def match_kernel(queries, cap, start, first, last, *refs):
     outs = refs[-queries:] if last else refs[-2:]
     refs = refs[: -queries] if last else refs[:-2]
     held, refs = refs[:queries], refs[queries:]
-    sums, keys = (refs[:2], refs[2:]) if last else (None, refs)
+    sums, keys = (None, refs) if first else (refs[:2], refs[2:])
     width = held[0].shape[2]
     diagonal = lax.broadcasted_iota(jnp.int32, (cap, cap), 0) == lax.broadcasted_iota(
         jnp.int32, (cap, cap), 1
     )
     for j in range(queries):
         query = held[j][:, :cap, :].reshape(2 * cap, width)
-        span = slice(j * 2 * cap, (j + 1) * 2 * cap)
+        span = slice((start + j) * 2 * cap, (start + j + 1) * 2 * cap)
         columns = []
         for part in range(2):
             line = jnp.broadcast_to(code_line(held[j], part, cap), (cap, cap))
@@ -167,10 +194,10 @@
                 weight.astype(jnp.bfloat16), key, preferred_element_type=jnp.float32
             ), mass
 
-        if last:
+        if first:
+            carry = jnp.zeros((2 * cap, width), jnp.float32), jnp.zeros((2 * cap, 1), jnp.float32)
+        else:
             carry = sums[0][span, :], sums[1][span, :]
-        else:
-            carry = jnp.zeros((2 * cap, width), jnp.float32), jnp.zeros((2 * cap, 1), jnp.float32)
         for key_ref in keys:
             pairs = key_ref.shape[0] // 2
             if pairs == 1:
@@ -188,9 +215,9 @@
             outs[1][span, :] = mass
 
 
-def match(held, keys, cap, sums=None):
+def match(held, keys, cap, sums=None, last=False, start=0):
     count, width = len(held), held[0].shape[2]
-    if sums is None:
+    if not last:
         shapes = [
             jax.ShapeDtypeStruct((count * 2 * cap, width), jnp.float32),
             jax.ShapeDtypeStruct((count * 2 * cap, 1), jnp.float32),
@@ -199,7 +226,7 @@
         shapes = [jax.ShapeDtypeStruct((2, cap, width), jnp.bfloat16)] * count
     operands = (*held, *(sums or ()), *keys)
     return pl.pallas_call(
-        functools.partial(match_kernel, count, cap, sums is not None),
+        functools.partial(match_kernel, count, cap, start, sums is None, last),
         in_specs=[pl.BlockSpec(memory_space=pltpu.VMEM)] * len(operands),
         out_specs=[pl.BlockSpec(memory_space=pltpu.VMEM)] * len(shapes),
         out_shape=shapes,
@@ -234,44 +261,48 @@
     chips = lax.axis_size("z_lo") * lax.axis_size("near")
     near, rest = lax.axis_size("near"), lax.axis_size("far")
     cap = 2 * row_count // chips
-    count = chips // 2
-    by_hops = sorted(range(chips), key=lambda d: -d.bit_count())
+    by_hops = sorted(range(chips), key=lambda d: (-(d // near), -d.bit_count()))
     flips = [[d for d in by_hops if d.bit_count() % 2 == odd] for odd in (1, 0)]
-    core = lax.axis_index("core")
-    spot = lax.axis_index(("z_lo", "near"))
-    table = jnp.array(flips, jnp.int32)
-    owners = spot ^ jnp.where(core == 0, table, table[::-1])
-
     def to_core(x):
         return lax.ppermute(x, "core", SWAP)
 
     def to_half(x):
         return lax.ppermute(x, "z_hi", SWAP)
 
-    def to_chip(x, j):
+    def to_chip(x, j, back=False):
         def number(c, s):
             return (s // near * 2 + c) * near + s % near
 
-        pairs = [
-            (number(c, s), number(c, s ^ flips[c][j])) for c in range(2) for s in range(chips)
-        ]
+        pairs = []
+        for s in range(chips):
+            stays = flips[1][j] == 0
+            pairs.append((number(0, s), number(1 if stays else 0, s ^ flips[0][j])))
+            pairs.append((number(1, s), number(0 if stays else 1, s ^ flips[1][j])))
+        if back:
+            pairs = [(target, origin) for origin, target in pairs]
         return lax.ppermute(x, ("z_lo", "core", "near"), pairs)
 
-    def spread(blocks):
-        messages = [to_chip(m, j) for j, m in enumerate(pack(owners, blocks, count, cap))]
-        keys = messages
+    def gathered(messages):
         if rest > 1:
-            keys = [lax.all_gather(m, "far", axis=0, tiled=True) for m in messages]
-        return messages, keys + [to_core(m) for m in keys]
+            return [lax.all_gather(m, "far", axis=0, tiled=True) for m in messages]
+        return messages
 
     block = scale(records, owner, subkey, source)
     far_block = to_half(block)
-    held, keys = spread((block, to_core(block)))
-    sums = match(held, keys, cap)
-    _, far_keys = spread((far_block, to_core(far_block)))
-    merged = match(held, far_keys, cap, sums)
-    returned = [to_chip(m, j) for j, m in enumerate(merged)]
-    places = place(owners, owner, count, cap)
+    places = place(owner, flips, cap)
+    held = [to_chip(m, j) for j, m in enumerate(pack((block, to_core(block)), flips, cap))]
+    far_block, places, held = lax.optimization_barrier((far_block, places, held))
+    near_keys = gathered(held)
+    near_keys = near_keys + [to_core(m) for m in near_keys]
+    far_messages = pack((far_block, to_core(far_block)), flips, cap)
+    near_keys, _ = lax.optimization_barrier((near_keys, far_messages[0]))
+    far_keys = gathered([to_chip(m, j) for j, m in enumerate(far_messages)])
+    sums = match(held, near_keys, cap)
+    sums, far_keys = lax.optimization_barrier((sums, far_keys))
+    swapped = [to_core(m) for m in far_keys]
+    sums = match(held, far_keys, cap, sums)
+    merged = match(held, swapped, cap, sums, last=True)
+    returned = [to_chip(m, j, back=True) for j, m in enumerate(merged)]
     return unpack(places, returned, [to_core(m) for m in returned], cap)
 
 

time: 60 us -> 52.5 us (0.88)
  starting transfers between devices: 28.1 us -> 20.8 us
  waiting for transfers between devices: 15.2 us -> 18.3 us
  local copies, waits for them, and re-layouts: 3.16 us -> 0.15 us
    ppermute x12, starting transfers between devices: 22.1 us -> 14.3 us  [to_chip(): return lax.ppermute(x, ('z_lo', 'core', 'near'), pairs)]
    unnamed x13 -> x3, local copies, waits for them, and re-layouts: 3.16 us -> 0.15 us
    ppermute x14, waiting for transfers between devices: 0.05 us -> 1.8 us  [to_core(): return lax.ppermute(x, 'core', SWAP)]
    ppermute x12, waiting for transfers between devices: 8.67 us -> 10.2 us  [to_chip(): return lax.ppermute(x, ('z_lo', 'core', 'near'), pairs)]
    pallas_call x6 -> x7, Pallas kernels: 11.8 us -> 11.7 us  [the longest x3 8.03 us: match(): pl.pallas_call(functools.partial(match_kernel, count, cap, start, sums is...]
  transfers between devices with their start and end apart: 27 -> 27, of which waited for: 10 -> 10; matrix products, arithmetic and copies ran while one was open for 0% -> 0% of each run, Pallas kernels for 13% -> 16%
where the time goes in v2:
time: 52.5 us; the launch traced here: 52.4 us
  starting transfers between devices  20.8 us (40%)
  waiting for transfers between devices  18.3 us (35%)
  Pallas kernels  13 us (25%)
    ppermute x12, starting transfers between devices, to_chip(): return lax.ppermute(x, ('z_lo', 'core', 'near'), pairs)  14.3 us
    ppermute x12, waiting for transfers between devices, to_chip(): return lax.ppermute(x, ('z_lo', 'core', 'near'), pairs)  10.2 us
    pallas_call x3, Pallas kernels, match(): pl.pallas_call(functools.partial(match_kernel, count, cap, start, sums is...  8.03 us
    ppermute x1, waiting for transfers between devices, to_half(): return lax.ppermute(x, 'z_hi', SWAP)  6.22 us
    ppermute x1, starting transfers between devices, to_half(): return lax.ppermute(x, 'z_hi', SWAP)  3.66 us
    ppermute x14, starting transfers between devices, to_core(): return lax.ppermute(x, 'core', SWAP)  2.9 us
    pallas_call x2, Pallas kernels, pack(): pl.pallas_call(functools.partial(pack_kernel, flips, cap), in_specs=[pl.B...  1.97 us
    ppermute x14, waiting for transfers between devices, to_core(): return lax.ppermute(x, 'core', SWAP)  1.8 us
  transfers between devices with their start and end apart: 27, of which 10 were waited for; matrix products, arithmetic and copies ran while one was open for 0% of the time, Pallas kernels for 16%

profile of v2, /device:TPU:0, one launch (start us, length us, event | category | flops | bytes accessed | tf_op | source)
XLA Modules:
  0.0 52.4 jit_solution(3993816200760304484)
XLA Ops:
  0.0 1.1 %shard_map.46.refs_0_ = bf16[520,256]{1,0:T(8,128)(2,1)S(1)} custom-call(bf16[512,256]{1,0:T(8,128)(2,1)} %rows_hbm.1, s32[1,512]{1,0:T(1,128)} %bitcast.3, s32[1,512]{1,0:T(1,128)} %bitcast.4, s32[1,512]{1,0:T(1,128)} %bitcast.5), custom_call_target="tpu_custom_call" | custom-call | tf_op jit(solution)/shard_map/pallas_call | solution.py:76
  1.2 0.5 collective-permute-start.1
  1.7 3.7 %collective-permute-start = (bf16[520,256]{1,0:T(8,128)(2,1)S(1)}, bf16[520,256]{1,0:T(8,128)(2,1)S(1)}, u32[]{:S(2)}, u32[]{:S(2)}) collective-permute-start(bf16[520,256]{1,0:T(8,128)(2,1)S(1)} %shard_map.46.refs_0_), channel_id=1, source_target_pairs={{0,16},{16,0},{1,17},{17,1},{2,18},{18,2},{3,19},{19,3},{4,20},{20... | collective-permute-start | bytes 798728 | tf_op jit(solution)/shard_map/ppermute | solution.py:270
  5.3 1.0 %shard_map.48 = (bf16[2,136,256]{2,1,0:T(8,128)(2,1)S(1)}, bf16[2,136,256]{2,1,0:T(8,128)(2,1)S(1)}, bf16[2,136,256]{2,1,0:T(8,128)(2,1)S(1)}, bf16[2,136,256]{2,1,0:T(8,128)(2,1)S(1)}) custom-call(bf16[520,256]{1,0:T(8,128)(2,1)S(1)} %shard_map.46.refs_0_, bf16[520,256]{1,0:T(8,128)(2,1)S(1)} %collective-permute-done.1.refs_1_), custom_call_target="tpu_custom_call" | custom-call | tf_op jit(solution)/shard_map/pallas_call | solution.py:121
  6.3 3.5 %collective-permute-start.2 = (bf16[2,136,256]{2,1,0:T(8,128)(2,1)S(1)}, bf16[2,136,256]{2,1,0:T(8,128)(2,1)S(1)}, u32[]{:S(2)}, u32[]{:S(2)}) collective-permute-start(bf16[2,136,256]{2,1,0:T(8,128)(2,1)S(1)} %get-tuple-element.41), channel_id=1, source_target_pairs={{0,11},{4,13},{1,10},{5,12},{2,9},{6,15},{3,8},{7,14},{8,3},{12,5}... | collective-permute-start | bytes 417800 | tf_op jit(solution)/shard_map/ppermute | solution.py:283
  10.3 0.5 %collective-permute-start.4 = (bf16[2,136,256]{2,1,0:T(8,128)(2,1)S(1)}, bf16[2,136,256]{2,1,0:T(8,128)(2,1)S(1)}, u32[]{:S(2)}, u32[]{:S(2)}) collective-permute-start(bf16[2,136,256]{2,1,0:T(8,128)(2,1)S(1)} %get-tuple-element.43), channel_id=1, source_target_pairs={{0,1},{4,7},{1,0},{5,6},{2,3},{6,5},{3,2},{7,4},{8,9},{12,15},{9,8... | collective-permute-start | bytes 417800 | tf_op jit(solution)/shard_map/ppermute | solution.py:283
  11.9 6.2 %collective-permute-done.refs_0_ = bf16[520,256]{1,0:T(8,128)(2,1)S(1)} collective-permute-done((bf16[520,256]{1,0:T(8,128)(2,1)S(1)}, bf16[520,256]{1,0:T(8,128)(2,1)S(1)}, u32[]{:S(2)}, u32[]{:S(2)}) %collective-permute-start) | collective-permute-done | bytes 266272 | tf_op jit(solution)/shard_map/ppermute | solution.py:270
  18.1 2.7 %collective-permute-done.3.refs_1_.refs_5_ = bf16[2,136,256]{2,1,0:T(8,128)(2,1)S(1)} collective-permute-done((bf16[2,136,256]{2,1,0:T(8,128)(2,1)S(1)}, bf16[2,136,256]{2,1,0:T(8,128)(2,1)S(1)}, u32[]{:S(2)}, u32[]{:S(2)}) %collective-permute-start.3) | collective-permute-done | bytes 139296 | tf_op jit(solution)/shard_map/ppermute | solution.py:283
  22.4 1.0 %shard_map.49 = (bf16[2,136,256]{2,1,0:T(8,128)(2,1)S(1)}, bf16[2,136,256]{2,1,0:T(8,128)(2,1)S(1)}, bf16[2,136,256]{2,1,0:T(8,128)(2,1)S(1)}, bf16[2,136,256]{2,1,0:T(8,128)(2,1)S(1)}) custom-call(bf16[520,256]{1,0:T(8,128)(2,1)S(1)} %collective-permute-done.refs_0_, bf16[520,256]{1,0:T(8,128)(2,1)S(1)} %collective-permute-done.10.refs_1_), custom_call_target="tpu_custom_call" | custom-call | tf_op jit(solution)/shard_map/pallas_call | solution.py:121
  23.5 0.8 %collective-permute-start.13 = (bf16[2,136,256]{2,1,0:T(8,128)(2,1)S(1)}, bf16[2,136,256]{2,1,0:T(8,128)(2,1)S(1)}, u32[]{:S(2)}, u32[]{:S(2)}) collective-permute-start(bf16[2,136,256]{2,1,0:T(8,128)(2,1)S(1)} %get-tuple-element.63), channel_id=1, source_target_pairs={{0,1},{4,7},{1,0},{5,6},{2,3},{6,5},{3,2},{7,4},{8,9},{12,15},{9,8... | collective-permute-start | bytes 417800 | tf_op jit(solution)/shard_map/ppermute | solution.py:283
  24.2 1.6 %collective-permute-start.14 = (bf16[2,136,256]{2,1,0:T(8,128)(2,1)S(1)}, bf16[2,136,256]{2,1,0:T(8,128)(2,1)S(1)}, u32[]{:S(2)}, u32[]{:S(2)}) collective-permute-start(bf16[2,136,256]{2,1,0:T(8,128)(2,1)S(1)} %get-tuple-element.64), channel_id=1, source_target_pairs={{0,6},{4,0},{1,7},{5,1},{2,4},{6,2},{3,5},{7,3},{8,14},{12,8},{9,1... | collective-permute-start | bytes 417800 | tf_op jit(solution)/shard_map/ppermute | solution.py:283
  25.8 2.6 %collective-permute-start.11 = (bf16[2,136,256]{2,1,0:T(8,128)(2,1)S(1)}, bf16[2,136,256]{2,1,0:T(8,128)(2,1)S(1)}, u32[]{:S(2)}, u32[]{:S(2)}) collective-permute-start(bf16[2,136,256]{2,1,0:T(8,128)(2,1)S(1)} %get-tuple-element.51), channel_id=1, source_target_pairs={{0,11},{4,13},{1,10},{5,12},{2,9},{6,15},{3,8},{7,14},{8,3},{12,5}... | collective-permute-start | bytes 417800 | tf_op jit(solution)/shard_map/ppermute | solution.py:283
  28.5 3.8 %shard_map.50 = (f32[1024,256]{1,0:T(8,128)S(1)}, f32[1024,1]{1,0:T(8,128)S(1)}) custom-call(bf16[2,136,256]{2,1,0:T(8,128)(2,1)S(1)} %collective-permute-done.2.refs_0_.refs_4_, bf16[2,136,256]{2,1,0:T(8,128)(2,1)S(1)} %collective-permute-done.3.refs_1_.refs_5_, bf16[2,136,256]{2,1,0:T(8,128)(2,1)S(1)} %collective-permute-done.4.refs_2_.refs_6_, ...), custom_call_target="tpu_custom_call" | custom-call | tf_op jit(solution)/shard_map/pallas_call | solution.py:228
  32.3 0.7 %collective-permute-done.13.refs_8_ = bf16[2,136,256]{2,1,0:T(8,128)(2,1)S(1)} collective-permute-done((bf16[2,136,256]{2,1,0:T(8,128)(2,1)S(1)}, bf16[2,136,256]{2,1,0:T(8,128)(2,1)S(1)}, u32[]{:S(2)}, u32[]{:S(2)}) %collective-permute-start.13) | collective-permute-done | bytes 139296 | tf_op jit(solution)/shard_map/ppermute | solution.py:283
  34.2 2.1 %shard_map.51 = (f32[1024,256]{1,0:T(8,128)S(1)}, f32[1024,1]{1,0:T(8,128)S(1)}) custom-call(bf16[2,136,256]{2,1,0:T(8,128)(2,1)S(1)} %collective-permute-done.2.refs_0_.refs_4_, bf16[2,136,256]{2,1,0:T(8,128)(2,1)S(1)} %collective-permute-done.3.refs_1_.refs_5_, bf16[2,136,256]{2,1,0:T(8,128)(2,1)S(1)} %collective-permute-done.4.refs_2_.refs_6_, ...), custom_call_target="tpu_custom_call" | custom-call | tf_op jit(solution)/shard_map/pallas_call | solution.py:228
  36.3 2.1 %shard_map.52 = (bf16[2,128,256]{2,1,0:T(8,128)(2,1)S(1)}, bf16[2,128,256]{2,1,0:T(8,128)(2,1)S(1)}, bf16[2,128,256]{2,1,0:T(8,128)(2,1)S(1)}, bf16[2,128,256]{2,1,0:T(8,128)(2,1)S(1)}) custom-call(bf16[2,136,256]{2,1,0:T(8,128)(2,1)S(1)} %collective-permute-done.2.refs_0_.refs_4_, bf16[2,136,256]{2,1,0:T(8,128)(2,1)S(1)} %collective-permute-done.3.refs_1_.refs_5_, ...), custom_call_target="tpu_custom_call" | custom-call | tf_op jit(solution)/shard_map/pallas_call | solution.py:228
  38.4 2.5 %collective-permute-start.19 = (bf16[2,128,256]{2,1,0:T(8,128)(2,1)S(1)}, bf16[2,128,256]{2,1,0:T(8,128)(2,1)S(1)}, u32[]{:S(2)}, u32[]{:S(2)}) collective-permute-start(bf16[2,128,256]{2,1,0:T(8,128)(2,1)S(1)} %get-tuple-element.73), channel_id=1, source_target_pairs={{11,0},{13,4},{10,1},{12,5},{9,2},{15,6},{8,3},{14,7},{3,8},{5,12}... | collective-permute-start | bytes 393224 | tf_op jit(solution)/shard_map/ppermute | solution.py:283
  40.9 1.2 %collective-permute-start.20 = (bf16[2,128,256]{2,1,0:T(8,128)(2,1)S(1)}, bf16[2,128,256]{2,1,0:T(8,128)(2,1)S(1)}, u32[]{:S(2)}, u32[]{:S(2)}) collective-permute-start(bf16[2,128,256]{2,1,0:T(8,128)(2,1)S(1)} %get-tuple-element.74), channel_id=1, source_target_pairs={{8,0},{14,4},{9,1},{15,5},{10,2},{12,6},{11,3},{13,7},{0,8},{6,12}... | collective-permute-start | bytes 393224 | tf_op jit(solution)/shard_map/ppermute | solution.py:283
  42.1 0.6 %collective-permute-start.21 = (bf16[2,128,256]{2,1,0:T(8,128)(2,1)S(1)}, bf16[2,128,256]{2,1,0:T(8,128)(2,1)S(1)}, u32[]{:S(2)}, u32[]{:S(2)}) collective-permute-start(bf16[2,128,256]{2,1,0:T(8,128)(2,1)S(1)} %get-tuple-element.75), channel_id=1, source_target_pairs={{1,0},{7,4},{0,1},{6,5},{3,2},{5,6},{2,3},{4,7},{9,8},{15,12},{8,9... | collective-permute-start | bytes 393224 | tf_op jit(solution)/shard_map/ppermute | solution.py:283
  42.7 4.5 %collective-permute-done.19.refs_0_ = bf16[2,128,256]{2,1,0:T(8,128)(2,1)S(1)} collective-permute-done((bf16[2,128,256]{2,1,0:T(8,128)(2,1)S(1)}, bf16[2,128,256]{2,1,0:T(8,128)(2,1)S(1)}, u32[]{:S(2)}, u32[]{:S(2)}) %collective-permute-start.19) | collective-permute-done | bytes 131104 | tf_op jit(solution)/shard_map/ppermute | solution.py:283
  47.8 0.6 %collective-permute-done.21.refs_2_ = bf16[2,128,256]{2,1,0:T(8,128)(2,1)S(1)} collective-permute-done((bf16[2,128,256]{2,1,0:T(8,128)(2,1)S(1)}, bf16[2,128,256]{2,1,0:T(8,128)(2,1)S(1)}, u32[]{:S(2)}, u32[]{:S(2)}) %collective-permute-start.21) | collective-permute-done | bytes 131104 | tf_op jit(solution)/shard_map/ppermute | solution.py:283
  48.4 1.3 %collective-permute-done.22.refs_3_ = bf16[2,128,256]{2,1,0:T(8,128)(2,1)S(1)} collective-permute-done((bf16[2,128,256]{2,1,0:T(8,128)(2,1)S(1)}, bf16[2,128,256]{2,1,0:T(8,128)(2,1)S(1)}, u32[]{:S(2)}, u32[]{:S(2)}) %collective-permute-start.22) | collective-permute-done | bytes 131104 | tf_op jit(solution)/shard_map/ppermute | solution.py:283
  49.7 1.3 %collective-permute-done.26.refs_7_ = bf16[2,128,256]{2,1,0:T(8,128)(2,1)S(1)} collective-permute-done((bf16[2,128,256]{2,1,0:T(8,128)(2,1)S(1)}, bf16[2,128,256]{2,1,0:T(8,128)(2,1)S(1)}, u32[]{:S(2)}, u32[]{:S(2)}) %collective-permute-start.26) | collective-permute-done | bytes 131104 | tf_op jit(solution)/shard_map/ppermute | solution.py:267
  51.1 1.3 %shard_map.53 = bf16[512,256]{1,0:T(8,128)(2,1)} custom-call(s32[512,1]{1,0:T(8,128)S(1)} %shard_map.47.place_ref, bf16[2,128,256]{2,1,0:T(8,128)(2,1)S(1)} %collective-permute-done.19.refs_0_, bf16[2,128,256]{2,1,0:T(8,128)(2,1)S(1)} %collective-permute-done.20.refs_1_, bf16[2,128,256]{2,1,0:T(8,128)(2,1)S(1)} %collective-permute-done.21.refs_2_, ...), custom_call_target="tpu_custom_call" | custom-call | tf_op jit(solution)/shard_map/pallas_call | solution.py:250
  (41 shorter events, 4.8 us)
Async XLA Ops:
  1.2 4.2 %collective-permute-start.1 = (bf16[520,256]{1,0:T(8,128)(2,1)S(1)}, bf16[520,256]{1,0:T(8,128)(2,1)S(1)}, u32[]{:S(2)}, u32[]{:S(2)}) collective-permute-start(bf16[520,256]{1,0:T(8,128)(2,1)S(1)} %shard_map.46.refs_0_), channel_id=1, source_target_pairs={{0,4},{4,0},{1,5},{5,1},{2,6},{6,2},{3,7},{7,3},{8,12},{12,8},{9,1... | collective-permute-start | bytes 798728 | tf_op jit(solution)/shard_map/ppermute | solution.py:267
  1.7 16.5 %collective-permute-start = (bf16[520,256]{1,0:T(8,128)(2,1)S(1)}, bf16[520,256]{1,0:T(8,128)(2,1)S(1)}, u32[]{:S(2)}, u32[]{:S(2)}) collective-permute-start(bf16[520,256]{1,0:T(8,128)(2,1)S(1)} %shard_map.46.refs_0_), channel_id=1, source_target_pairs={{0,16},{16,0},{1,17},{17,1},{2,18},{18,2},{3,19},{19,3},{4,20},{20... | collective-permute-start | bytes 798728 | tf_op jit(solution)/shard_map/ppermute | solution.py:270
  6.3 11.8 %collective-permute-start.2 = (bf16[2,136,256]{2,1,0:T(8,128)(2,1)S(1)}, bf16[2,136,256]{2,1,0:T(8,128)(2,1)S(1)}, u32[]{:S(2)}, u32[]{:S(2)}) collective-permute-start(bf16[2,136,256]{2,1,0:T(8,128)(2,1)S(1)} %get-tuple-element.41), channel_id=1, source_target_pairs={{0,11},{4,13},{1,10},{5,12},{2,9},{6,15},{3,8},{7,14},{8,3},{12,5}... | collective-permute-start | bytes 417800 | tf_op jit(solution)/shard_map/ppermute | solution.py:283
  9.9 11.0 %collective-permute-start.3 = (bf16[2,136,256]{2,1,0:T(8,128)(2,1)S(1)}, bf16[2,136,256]{2,1,0:T(8,128)(2,1)S(1)}, u32[]{:S(2)}, u32[]{:S(2)}) collective-permute-start(bf16[2,136,256]{2,1,0:T(8,128)(2,1)S(1)} %get-tuple-element.42), channel_id=1, source_target_pairs={{0,8},{4,14},{1,9},{5,15},{2,10},{6,12},{3,11},{7,13},{8,0},{12,6}... | collective-permute-start | bytes 417800 | tf_op jit(solution)/shard_map/ppermute | solution.py:283
  10.3 10.5 %collective-permute-start.4 = (bf16[2,136,256]{2,1,0:T(8,128)(2,1)S(1)}, bf16[2,136,256]{2,1,0:T(8,128)(2,1)S(1)}, u32[]{:S(2)}, u32[]{:S(2)}) collective-permute-start(bf16[2,136,256]{2,1,0:T(8,128)(2,1)S(1)} %get-tuple-element.43), channel_id=1, source_target_pairs={{0,1},{4,7},{1,0},{5,6},{2,3},{6,5},{3,2},{7,4},{8,9},{12,15},{9,8... | collective-permute-start | bytes 417800 | tf_op jit(solution)/shard_map/ppermute | solution.py:283
  10.8 10.0 %collective-permute-start.5 = (bf16[2,136,256]{2,1,0:T(8,128)(2,1)S(1)}, bf16[2,136,256]{2,1,0:T(8,128)(2,1)S(1)}, u32[]{:S(2)}, u32[]{:S(2)}) collective-permute-start(bf16[2,136,256]{2,1,0:T(8,128)(2,1)S(1)} %get-tuple-element.44), channel_id=1, source_target_pairs={{0,6},{4,0},{1,7},{5,1},{2,4},{6,2},{3,5},{7,3},{8,14},{12,8},{9,1... | collective-permute-start | bytes 417800 | tf_op jit(solution)/shard_map/ppermute | solution.py:283
  20.9 2.6 %collective-permute-start.6 = (bf16[2,136,256]{2,1,0:T(8,128)(2,1)S(1)}, bf16[2,136,256]{2,1,0:T(8,128)(2,1)S(1)}, u32[]{:S(2)}, u32[]{:S(2)}) collective-permute-start(bf16[2,136,256]{2,1,0:T(8,128)(2,1)S(1)} %collective-permute-done.2.refs_0_.refs_4_), channel_id=1, source_target_pairs={{0,4},{4,0},{1,5},{5,1},{2,6},{6,2},{3,7},{7,3},{8,12},{12,8},{9,1... | collective-permute-start | bytes 417800 | tf_op jit(solution)/shard_map/ppermute | solution.py:267
  21.4 2.9 %collective-permute-start.7 = (bf16[2,136,256]{2,1,0:T(8,128)(2,1)S(1)}, bf16[2,136,256]{2,1,0:T(8,128)(2,1)S(1)}, u32[]{:S(2)}, u32[]{:S(2)}) collective-permute-start(bf16[2,136,256]{2,1,0:T(8,128)(2,1)S(1)} %collective-permute-done.3.refs_1_.refs_5_), channel_id=1, source_target_pairs={{0,4},{4,0},{1,5},{5,1},{2,6},{6,2},{3,7},{7,3},{8,12},{12,8},{9,1... | collective-permute-start | bytes 417800 | tf_op jit(solution)/shard_map/ppermute | solution.py:267
  21.4 4.4 %collective-permute-start.8 = (bf16[2,136,256]{2,1,0:T(8,128)(2,1)S(1)}, bf16[2,136,256]{2,1,0:T(8,128)(2,1)S(1)}, u32[]{:S(2)}, u32[]{:S(2)}) collective-permute-start(bf16[2,136,256]{2,1,0:T(8,128)(2,1)S(1)} %collective-permute-done.4.refs_2_.refs_6_), channel_id=1, source_target_pairs={{0,4},{4,0},{1,5},{5,1},{2,6},{6,2},{3,7},{7,3},{8,12},{12,8},{9,1... | collective-permute-start | bytes 417800 | tf_op jit(solution)/shard_map/ppermute | solution.py:267
  21.9 6.6 %collective-permute-start.9 = (bf16[2,136,256]{2,1,0:T(8,128)(2,1)S(1)}, bf16[2,136,256]{2,1,0:T(8,128)(2,1)S(1)}, u32[]{:S(2)}, u32[]{:S(2)}) collective-permute-start(bf16[2,136,256]{2,1,0:T(8,128)(2,1)S(1)} %collective-permute-done.5.refs_3_.refs_7_), channel_id=1, source_target_pairs={{0,4},{4,0},{1,5},{5,1},{2,6},{6,2},{3,7},{7,3},{8,12},{12,8},{9,1... | collective-permute-start | bytes 417800 | tf_op jit(solution)/shard_map/ppermute | solution.py:267
  23.4 8.9 %collective-permute-start.12 = (bf16[2,136,256]{2,1,0:T(8,128)(2,1)S(1)}, bf16[2,136,256]{2,1,0:T(8,128)(2,1)S(1)}, u32[]{:S(2)}, u32[]{:S(2)}) collective-permute-start(bf16[2,136,256]{2,1,0:T(8,128)(2,1)S(1)} %get-tuple-element.62), channel_id=1, source_target_pairs={{0,8},{4,14},{1,9},{5,15},{2,10},{6,12},{3,11},{7,13},{8,0},{12,6}... | collective-permute-start | bytes 417800 | tf_op jit(solution)/shard_map/ppermute | solution.py:283
  23.5 9.5 %collective-permute-start.13 = (bf16[2,136,256]{2,1,0:T(8,128)(2,1)S(1)}, bf16[2,136,256]{2,1,0:T(8,128)(2,1)S(1)}, u32[]{:S(2)}, u32[]{:S(2)}) collective-permute-start(bf16[2,136,256]{2,1,0:T(8,128)(2,1)S(1)} %get-tuple-element.63), channel_id=1, source_target_pairs={{0,1},{4,7},{1,0},{5,6},{2,3},{6,5},{3,2},{7,4},{8,9},{12,15},{9,8... | collective-permute-start | bytes 417800 | tf_op jit(solution)/shard_map/ppermute | solution.py:283
  24.2 8.8 %collective-permute-start.14 = (bf16[2,136,256]{2,1,0:T(8,128)(2,1)S(1)}, bf16[2,136,256]{2,1,0:T(8,128)(2,1)S(1)}, u32[]{:S(2)}, u32[]{:S(2)}) collective-permute-start(bf16[2,136,256]{2,1,0:T(8,128)(2,1)S(1)} %get-tuple-element.64), channel_id=1, source_target_pairs={{0,6},{4,0},{1,7},{5,1},{2,4},{6,2},{3,5},{7,3},{8,14},{12,8},{9,1... | collective-permute-start | bytes 417800 | tf_op jit(solution)/shard_map/ppermute | solution.py:283
  25.8 7.3 %collective-permute-start.11 = (bf16[2,136,256]{2,1,0:T(8,128)(2,1)S(1)}, bf16[2,136,256]{2,1,0:T(8,128)(2,1)S(1)}, u32[]{:S(2)}, u32[]{:S(2)}) collective-permute-start(bf16[2,136,256]{2,1,0:T(8,128)(2,1)S(1)} %get-tuple-element.51), channel_id=1, source_target_pairs={{0,11},{4,13},{1,10},{5,12},{2,9},{6,15},{3,8},{7,14},{8,3},{12,5}... | collective-permute-start | bytes 417800 | tf_op jit(solution)/shard_map/ppermute | solution.py:283
  33.1 3.1 %collective-permute-start.15 = (bf16[2,136,256]{2,1,0:T(8,128)(2,1)S(1)}, bf16[2,136,256]{2,1,0:T(8,128)(2,1)S(1)}, u32[]{:S(2)}, u32[]{:S(2)}) collective-permute-start(bf16[2,136,256]{2,1,0:T(8,128)(2,1)S(1)} %collective-permute-done.11.refs_6_), channel_id=1, source_target_pairs={{0,4},{4,0},{1,5},{5,1},{2,6},{6,2},{3,7},{7,3},{8,12},{12,8},{9,1... | collective-permute-start | bytes 417800 | tf_op jit(solution)/shard_map/ppermute | solution.py:267
  33.1 3.1 %collective-permute-start.16 = (bf16[2,136,256]{2,1,0:T(8,128)(2,1)S(1)}, bf16[2,136,256]{2,1,0:T(8,128)(2,1)S(1)}, u32[]{:S(2)}, u32[]{:S(2)}) collective-permute-start(bf16[2,136,256]{2,1,0:T(8,128)(2,1)S(1)} %collective-permute-done.12.refs_7_), channel_id=1, source_target_pairs={{0,4},{4,0},{1,5},{5,1},{2,6},{6,2},{3,7},{7,3},{8,12},{12,8},{9,1... | collective-permute-start | bytes 417800 | tf_op jit(solution)/shard_map/ppermute | solution.py:267
  33.6 2.6 %collective-permute-start.17 = (bf16[2,136,256]{2,1,0:T(8,128)(2,1)S(1)}, bf16[2,136,256]{2,1,0:T(8,128)(2,1)S(1)}, u32[]{:S(2)}, u32[]{:S(2)}) collective-permute-start(bf16[2,136,256]{2,1,0:T(8,128)(2,1)S(1)} %collective-permute-done.13.refs_8_), channel_id=1, source_target_pairs={{0,4},{4,0},{1,5},{5,1},{2,6},{6,2},{3,7},{7,3},{8,12},{12,8},{9,1... | collective-permute-start | bytes 417800 | tf_op jit(solution)/shard_map/ppermute | solution.py:267
  33.6 2.6 %collective-permute-start.18 = (bf16[2,136,256]{2,1,0:T(8,128)(2,1)S(1)}, bf16[2,136,256]{2,1,0:T(8,128)(2,1)S(1)}, u32[]{:S(2)}, u32[]{:S(2)}) collective-permute-start(bf16[2,136,256]{2,1,0:T(8,128)(2,1)S(1)} %collective-permute-done.14.refs_9_), channel_id=1, source_target_pairs={{0,4},{4,0},{1,5},{5,1},{2,6},{6,2},{3,7},{7,3},{8,12},{12,8},{9,1... | collective-permute-start | bytes 417800 | tf_op jit(solution)/shard_map/ppermute | solution.py:267
  38.4 8.8 %collective-permute-start.19 = (bf16[2,128,256]{2,1,0:T(8,128)(2,1)S(1)}, bf16[2,128,256]{2,1,0:T(8,128)(2,1)S(1)}, u32[]{:S(2)}, u32[]{:S(2)}) collective-permute-start(bf16[2,128,256]{2,1,0:T(8,128)(2,1)S(1)} %get-tuple-element.73), channel_id=1, source_target_pairs={{11,0},{13,4},{10,1},{12,5},{9,2},{15,6},{8,3},{14,7},{3,8},{5,12}... | collective-permute-start | bytes 393224 | tf_op jit(solution)/shard_map/ppermute | solution.py:283
  40.9 6.6 %collective-permute-start.20 = (bf16[2,128,256]{2,1,0:T(8,128)(2,1)S(1)}, bf16[2,128,256]{2,1,0:T(8,128)(2,1)S(1)}, u32[]{:S(2)}, u32[]{:S(2)}) collective-permute-start(bf16[2,128,256]{2,1,0:T(8,128)(2,1)S(1)} %get-tuple-element.74), channel_id=1, source_target_pairs={{8,0},{14,4},{9,1},{15,5},{10,2},{12,6},{11,3},{13,7},{0,8},{6,12}... | collective-permute-start | bytes 393224 | tf_op jit(solution)/shard_map/ppermute | solution.py:283
  42.1 6.3 %collective-permute-start.21 = (bf16[2,128,256]{2,1,0:T(8,128)(2,1)S(1)}, bf16[2,128,256]{2,1,0:T(8,128)(2,1)S(1)}, u32[]{:S(2)}, u32[]{:S(2)}) collective-permute-start(bf16[2,128,256]{2,1,0:T(8,128)(2,1)S(1)} %get-tuple-element.75), channel_id=1, source_target_pairs={{1,0},{7,4},{0,1},{6,5},{3,2},{5,6},{2,3},{4,7},{9,8},{15,12},{8,9... | collective-permute-start | bytes 393224 | tf_op jit(solution)/shard_map/ppermute | solution.py:283
  42.7 7.0 %collective-permute-start.22 = (bf16[2,128,256]{2,1,0:T(8,128)(2,1)S(1)}, bf16[2,128,256]{2,1,0:T(8,128)(2,1)S(1)}, u32[]{:S(2)}, u32[]{:S(2)}) collective-permute-start(bf16[2,128,256]{2,1,0:T(8,128)(2,1)S(1)} %get-tuple-element.76), channel_id=1, source_target_pairs={{6,0},{0,4},{7,1},{1,5},{4,2},{2,6},{5,3},{3,7},{14,8},{8,12},{15,... | collective-permute-start | bytes 393224 | tf_op jit(solution)/shard_map/ppermute | solution.py:283
  47.3 2.5 %collective-permute-start.23 = (bf16[2,128,256]{2,1,0:T(8,128)(2,1)S(1)}, bf16[2,128,256]{2,1,0:T(8,128)(2,1)S(1)}, u32[]{:S(2)}, u32[]{:S(2)}) collective-permute-start(bf16[2,128,256]{2,1,0:T(8,128)(2,1)S(1)} %collective-permute-done.19.refs_0_), channel_id=1, source_target_pairs={{0,4},{4,0},{1,5},{5,1},{2,6},{6,2},{3,7},{7,3},{8,12},{12,8},{9,1... | collective-permute-start | bytes 393224 | tf_op jit(solution)/shard_map/ppermute | solution.py:267
  47.5 2.2 %collective-permute-start.24 = (bf16[2,128,256]{2,1,0:T(8,128)(2,1)S(1)}, bf16[2,128,256]{2,1,0:T(8,128)(2,1)S(1)}, u32[]{:S(2)}, u32[]{:S(2)}) collective-permute-start(bf16[2,128,256]{2,1,0:T(8,128)(2,1)S(1)} %collective-permute-done.20.refs_1_), channel_id=1, source_target_pairs={{0,4},{4,0},{1,5},{5,1},{2,6},{6,2},{3,7},{7,3},{8,12},{12,8},{9,1... | collective-permute-start | bytes 393224 | tf_op jit(solution)/shard_map/ppermute | solution.py:267
  (4 other events, 5.6 us)

commit v3 on v2

--- a/solution.py
+++ b/solution.py
@@ -234,26 +234,28 @@
     )(*operands)
 
 
-def unpack_kernel(count, cap, place_ref, *refs):
-    mine, sibling, out_ref = refs[:count], refs[count : 2 * count], refs[-1]
+def unpack_kernel(spots, cap, more, place_ref, *refs):
+    blocks, out_ref = refs[: len(spots)], refs[-1]
     rows = out_ref.shape[0]
-    slot = lax.broadcasted_iota(jnp.int32, (rows, 2 * count * cap), 1)
-    picks = jnp.where(slot == place_ref[...], 1.0, 0.0).astype(jnp.bfloat16)
-    blocks = [m[0] for m in mine] + [m[1] for m in sibling]
-    out_ref[...] = jnp.dot(
-        picks, jnp.concatenate(blocks, axis=0), preferred_element_type=jnp.float32
+    slot = lax.broadcasted_iota(jnp.int32, (rows, cap), 1)
+    picks = [jnp.where(slot + i * cap == place_ref[...], 1.0, 0.0).astype(jnp.bfloat16) for i, _ in spots]
+    found = jnp.dot(
+        jnp.concatenate(picks, axis=1),
+        jnp.concatenate([ref[part] for ref, (_, part) in zip(blocks, spots)], axis=0),
+        preferred_element_type=jnp.float32,
     ).astype(jnp.bfloat16)
-
-
-def unpack(places, mine, sibling, cap):
-    count, width = len(mine), mine[0].shape[2]
-    return pl.pallas_call(
-        functools.partial(unpack_kernel, count, cap),
-        in_specs=[pl.BlockSpec(memory_space=pltpu.VMEM)] * (2 * count + 1),
+    out_ref[...] = refs[len(spots)][...] + found if more else found
+
+
+def unpack(places, blocks, spots, cap, earlier=None):
+    operands = (places, *blocks, *(() if earlier is None else (earlier,)))
+    return pl.pallas_call(
+        functools.partial(unpack_kernel, spots, cap, earlier is not None),
+        in_specs=[pl.BlockSpec(memory_space=pltpu.VMEM)] * len(operands),
         out_specs=pl.BlockSpec(memory_space=pltpu.VMEM),
-        out_shape=jax.ShapeDtypeStruct((places.shape[0], width), jnp.bfloat16),
-        compiler_params=pltpu.CompilerParams(vmem_limit_bytes=VMEM_LIMIT),
-    )(places, *mine, *sibling)
+        out_shape=jax.ShapeDtypeStruct((places.shape[0], blocks[0].shape[2]), jnp.bfloat16),
+        compiler_params=pltpu.CompilerParams(vmem_limit_bytes=VMEM_LIMIT),
+    )(*operands)
 
 
 def shards(records, owner, subkey, source):
@@ -301,9 +303,15 @@
     sums, far_keys = lax.optimization_barrier((sums, far_keys))
     swapped = [to_core(m) for m in far_keys]
     sums = match(held, far_keys, cap, sums)
-    merged = match(held, swapped, cap, sums, last=True)
+    half = len(held) // 2
+    merged = match(held[:half], swapped, cap, sums, True)
+    sums, merged = lax.optimization_barrier((sums, merged))
+    merged = merged + match(held[half:], swapped, cap, sums, True, half)
     returned = [to_chip(m, j, back=True) for j, m in enumerate(merged)]
-    return unpack(places, returned, [to_core(m) for m in returned], cap)
+    count = len(returned)
+    swapped = [to_core(m) for m in returned]
+    early = unpack(places, returned, [(j, 0) for j in range(count)], cap)
+    return unpack(places, swapped, [(count + j, 1) for j in range(count)], cap, early)
 
 
 def solution(mesh):

time: 52.5 us -> 51.4 us (0.979)
  waiting for transfers between devices: 18.3 us -> 16.9 us
    ppermute x12, waiting for transfers between devices: 10.2 us -> 9.19 us  [to_chip(): return lax.ppermute(x, ('z_lo', 'core', 'near'), pairs)]
    pallas_call x3 -> x4, Pallas kernels: 8.03 us -> 8.39 us  [match(): pl.pallas_call(functools.partial(match_kernel, count, cap, start, sums is...]
    pallas_call x1 -> x2, Pallas kernels: 1.31 us -> 1.38 us  [unpack(): pl.pallas_call(functools.partial(unpack_kernel, spots, cap, earlier is no...]
  transfers between devices with their start and end apart: 27 -> 27, of which waited for: 10 -> 11; matrix products, arithmetic and copies ran while one was open for 0% -> 0% of each run, Pallas kernels for 16% -> 19%
where the time goes in v3:
time: 51.4 us; the launch traced here: 51.2 us
  starting transfers between devices  20.6 us (40%)
  waiting for transfers between devices  16.9 us (33%)
  Pallas kernels  13.4 us (26%)
    ppermute x12, starting transfers between devices, to_chip(): return lax.ppermute(x, ('z_lo', 'core', 'near'), pairs)  14.4 us
    ppermute x12, waiting for transfers between devices, to_chip(): return lax.ppermute(x, ('z_lo', 'core', 'near'), pairs)  9.19 us
    pallas_call x4, Pallas kernels, match(): pl.pallas_call(functools.partial(match_kernel, count, cap, start, sums is...  8.39 us
    ppermute x1, waiting for transfers between devices, to_half(): return lax.ppermute(x, 'z_hi', SWAP)  6.22 us
    ppermute x1, starting transfers between devices, to_half(): return lax.ppermute(x, 'z_hi', SWAP)  3.66 us
    ppermute x14, starting transfers between devices, to_core(): return lax.ppermute(x, 'core', SWAP)  2.64 us
    pallas_call x2, Pallas kernels, pack(): pl.pallas_call(functools.partial(pack_kernel, flips, cap), in_specs=[pl.B...  1.97 us
    ppermute x14, waiting for transfers between devices, to_core(): return lax.ppermute(x, 'core', SWAP)  1.46 us
  transfers between devices with their start and end apart: 27, of which 11 were waited for; matrix products, arithmetic and copies ran while one was open for 0% of the time, Pallas kernels for 19%

profile of v3, /device:TPU:0, one launch (start us, length us, event | category | flops | bytes accessed | tf_op | source)
XLA Modules:
  0.0 51.2 jit_solution(5975787561583201061)
XLA Ops:
  0.0 1.1 %shard_map.46.refs_0_ = bf16[520,256]{1,0:T(8,128)(2,1)S(1)} custom-call(bf16[512,256]{1,0:T(8,128)(2,1)} %rows_hbm.1, s32[1,512]{1,0:T(1,128)} %bitcast.3, s32[1,512]{1,0:T(1,128)} %bitcast.4, s32[1,512]{1,0:T(1,128)} %bitcast.5), custom_call_target="tpu_custom_call" | custom-call | tf_op jit(solution)/shard_map/pallas_call | solution.py:76
  1.7 3.7 %collective-permute-start = (bf16[520,256]{1,0:T(8,128)(2,1)S(1)}, bf16[520,256]{1,0:T(8,128)(2,1)S(1)}, u32[]{:S(2)}, u32[]{:S(2)}) collective-permute-start(bf16[520,256]{1,0:T(8,128)(2,1)S(1)} %shard_map.46.refs_0_), channel_id=1, source_target_pairs={{0,16},{16,0},{1,17},{17,1},{2,18},{18,2},{3,19},{19,3},{4,20},{20... | collective-permute-start | bytes 798728 | tf_op jit(solution)/shard_map/ppermute | solution.py:272
  5.3 1.0 %shard_map.48 = (bf16[2,136,256]{2,1,0:T(8,128)(2,1)S(1)}, bf16[2,136,256]{2,1,0:T(8,128)(2,1)S(1)}, bf16[2,136,256]{2,1,0:T(8,128)(2,1)S(1)}, bf16[2,136,256]{2,1,0:T(8,128)(2,1)S(1)}) custom-call(bf16[520,256]{1,0:T(8,128)(2,1)S(1)} %shard_map.46.refs_0_, bf16[520,256]{1,0:T(8,128)(2,1)S(1)} %collective-permute-done.1.refs_1_), custom_call_target="tpu_custom_call" | custom-call | tf_op jit(solution)/shard_map/pallas_call | solution.py:121
  6.3 3.5 %collective-permute-start.2 = (bf16[2,136,256]{2,1,0:T(8,128)(2,1)S(1)}, bf16[2,136,256]{2,1,0:T(8,128)(2,1)S(1)}, u32[]{:S(2)}, u32[]{:S(2)}) collective-permute-start(bf16[2,136,256]{2,1,0:T(8,128)(2,1)S(1)} %get-tuple-element.45), channel_id=1, source_target_pairs={{0,11},{4,13},{1,10},{5,12},{2,9},{6,15},{3,8},{7,14},{8,3},{12,5}... | collective-permute-start | bytes 417800 | tf_op jit(solution)/shard_map/ppermute | solution.py:285
  11.9 6.2 %collective-permute-done.refs_0_ = bf16[520,256]{1,0:T(8,128)(2,1)S(1)} collective-permute-done((bf16[520,256]{1,0:T(8,128)(2,1)S(1)}, bf16[520,256]{1,0:T(8,128)(2,1)S(1)}, u32[]{:S(2)}, u32[]{:S(2)}) %collective-permute-start) | collective-permute-done | bytes 266272 | tf_op jit(solution)/shard_map/ppermute | solution.py:272
  18.1 2.7 %collective-permute-done.3.refs_1_.refs_5_ = bf16[2,136,256]{2,1,0:T(8,128)(2,1)S(1)} collective-permute-done((bf16[2,136,256]{2,1,0:T(8,128)(2,1)S(1)}, bf16[2,136,256]{2,1,0:T(8,128)(2,1)S(1)}, u32[]{:S(2)}, u32[]{:S(2)}) %collective-permute-start.3) | collective-permute-done | bytes 139296 | tf_op jit(solution)/shard_map/ppermute | solution.py:285
  22.4 1.0 %shard_map.49 = (bf16[2,136,256]{2,1,0:T(8,128)(2,1)S(1)}, bf16[2,136,256]{2,1,0:T(8,128)(2,1)S(1)}, bf16[2,136,256]{2,1,0:T(8,128)(2,1)S(1)}, bf16[2,136,256]{2,1,0:T(8,128)(2,1)S(1)}) custom-call(bf16[520,256]{1,0:T(8,128)(2,1)S(1)} %collective-permute-done.refs_0_, bf16[520,256]{1,0:T(8,128)(2,1)S(1)} %collective-permute-done.10.refs_1_), custom_call_target="tpu_custom_call" | custom-call | tf_op jit(solution)/shard_map/pallas_call | solution.py:121
  23.5 0.8 %collective-permute-start.13 = (bf16[2,136,256]{2,1,0:T(8,128)(2,1)S(1)}, bf16[2,136,256]{2,1,0:T(8,128)(2,1)S(1)}, u32[]{:S(2)}, u32[]{:S(2)}) collective-permute-start(bf16[2,136,256]{2,1,0:T(8,128)(2,1)S(1)} %get-tuple-element.67), channel_id=1, source_target_pairs={{0,1},{4,7},{1,0},{5,6},{2,3},{6,5},{3,2},{7,4},{8,9},{12,15},{9,8... | collective-permute-start | bytes 417800 | tf_op jit(solution)/shard_map/ppermute | solution.py:285
  24.2 1.6 %collective-permute-start.14 = (bf16[2,136,256]{2,1,0:T(8,128)(2,1)S(1)}, bf16[2,136,256]{2,1,0:T(8,128)(2,1)S(1)}, u32[]{:S(2)}, u32[]{:S(2)}) collective-permute-start(bf16[2,136,256]{2,1,0:T(8,128)(2,1)S(1)} %get-tuple-element.68), channel_id=1, source_target_pairs={{0,6},{4,0},{1,7},{5,1},{2,4},{6,2},{3,5},{7,3},{8,14},{12,8},{9,1... | collective-permute-start | bytes 417800 | tf_op jit(solution)/shard_map/ppermute | solution.py:285
  25.8 2.6 %collective-permute-start.11 = (bf16[2,136,256]{2,1,0:T(8,128)(2,1)S(1)}, bf16[2,136,256]{2,1,0:T(8,128)(2,1)S(1)}, u32[]{:S(2)}, u32[]{:S(2)}) collective-permute-start(bf16[2,136,256]{2,1,0:T(8,128)(2,1)S(1)} %get-tuple-element.55), channel_id=1, source_target_pairs={{0,11},{4,13},{1,10},{5,12},{2,9},{6,15},{3,8},{7,14},{8,3},{12,5}... | collective-permute-start | bytes 417800 | tf_op jit(solution)/shard_map/ppermute | solution.py:285
  28.5 3.8 %shard_map.50 = (f32[1024,256]{1,0:T(8,128)S(1)}, f32[1024,1]{1,0:T(8,128)S(1)}) custom-call(bf16[2,136,256]{2,1,0:T(8,128)(2,1)S(1)} %collective-permute-done.2.refs_0_.refs_4_, bf16[2,136,256]{2,1,0:T(8,128)(2,1)S(1)} %collective-permute-done.3.refs_1_.refs_5_, bf16[2,136,256]{2,1,0:T(8,128)(2,1)S(1)} %collective-permute-done.4.refs_2_.refs_6_.refs_0_, ...), custom_call_target="tpu_custom_call" | custom-call | tf_op jit(solution)/shard_map/pallas_call | solution.py:228
  32.3 0.7 %collective-permute-done.13.refs_8_ = bf16[2,136,256]{2,1,0:T(8,128)(2,1)S(1)} collective-permute-done((bf16[2,136,256]{2,1,0:T(8,128)(2,1)S(1)}, bf16[2,136,256]{2,1,0:T(8,128)(2,1)S(1)}, u32[]{:S(2)}, u32[]{:S(2)}) %collective-permute-start.13) | collective-permute-done | bytes 139296 | tf_op jit(solution)/shard_map/ppermute | solution.py:285
  34.2 2.1 %shard_map.51 = (f32[1024,256]{1,0:T(8,128)S(1)}, f32[1024,1]{1,0:T(8,128)S(1)}) custom-call(bf16[2,136,256]{2,1,0:T(8,128)(2,1)S(1)} %collective-permute-done.2.refs_0_.refs_4_, bf16[2,136,256]{2,1,0:T(8,128)(2,1)S(1)} %collective-permute-done.3.refs_1_.refs_5_, bf16[2,136,256]{2,1,0:T(8,128)(2,1)S(1)} %collective-permute-done.4.refs_2_.refs_6_.refs_0_, ...), custom_call_target="tpu_custom_call" | custom-call | tf_op jit(solution)/shard_map/pallas_call | solution.py:228
  36.3 1.3 %shard_map.52 = (bf16[2,128,256]{2,1,0:T(8,128)(2,1)S(1)}, bf16[2,128,256]{2,1,0:T(8,128)(2,1)S(1)}) custom-call(bf16[2,136,256]{2,1,0:T(8,128)(2,1)S(1)} %collective-permute-done.2.refs_0_.refs_4_, bf16[2,136,256]{2,1,0:T(8,128)(2,1)S(1)} %collective-permute-done.3.refs_1_.refs_5_, f32[1024,256]{1,0:T(8,128)S(1)} %get-tuple-element.81.refs_2_, ...), custom_call_target="tpu_custom_call" | custom-call | tf_op jit(solution)/shard_map/pallas_call | solution.py:228
  37.5 2.5 %collective-permute-start.19 = (bf16[2,128,256]{2,1,0:T(8,128)(2,1)S(1)}, bf16[2,128,256]{2,1,0:T(8,128)(2,1)S(1)}, u32[]{:S(2)}, u32[]{:S(2)}) collective-permute-start(bf16[2,128,256]{2,1,0:T(8,128)(2,1)S(1)} %get-tuple-element.79), channel_id=1, source_target_pairs={{11,0},{13,4},{10,1},{12,5},{9,2},{15,6},{8,3},{14,7},{3,8},{5,12}... | collective-permute-start | bytes 393224 | tf_op jit(solution)/shard_map/ppermute | solution.py:285
  40.0 1.2 %collective-permute-start.21 = (bf16[2,128,256]{2,1,0:T(8,128)(2,1)S(1)}, bf16[2,128,256]{2,1,0:T(8,128)(2,1)S(1)}, u32[]{:S(2)}, u32[]{:S(2)}) collective-permute-start(bf16[2,128,256]{2,1,0:T(8,128)(2,1)S(1)} %get-tuple-element.80), channel_id=1, source_target_pairs={{8,0},{14,4},{9,1},{15,5},{10,2},{12,6},{11,3},{13,7},{0,8},{6,12}... | collective-permute-start | bytes 393224 | tf_op jit(solution)/shard_map/ppermute | solution.py:285
  41.2 1.3 %shard_map.53 = (bf16[2,128,256]{2,1,0:T(8,128)(2,1)S(1)}, bf16[2,128,256]{2,1,0:T(8,128)(2,1)S(1)}) custom-call(bf16[2,136,256]{2,1,0:T(8,128)(2,1)S(1)} %collective-permute-done.4.refs_2_.refs_6_.refs_0_, bf16[2,136,256]{2,1,0:T(8,128)(2,1)S(1)} %collective-permute-done.5.refs_3_.refs_7_.refs_1_, f32[1024,256]{1,0:T(8,128)S(1)} %get-tuple-element.81.refs_2_, ...), custom_call_target="tpu_custom_call" | custom-call | tf_op jit(solution)/shard_map/pallas_call | solution.py:228
  42.4 0.7 %collective-permute-start.23 = (bf16[2,128,256]{2,1,0:T(8,128)(2,1)S(1)}, bf16[2,128,256]{2,1,0:T(8,128)(2,1)S(1)}, u32[]{:S(2)}, u32[]{:S(2)}) collective-permute-start(bf16[2,128,256]{2,1,0:T(8,128)(2,1)S(1)} %get-tuple-element.83), channel_id=1, source_target_pairs={{1,0},{7,4},{0,1},{6,5},{3,2},{5,6},{2,3},{4,7},{9,8},{15,12},{8,9... | collective-permute-start | bytes 393224 | tf_op jit(solution)/shard_map/ppermute | solution.py:285
  43.2 2.6 %collective-permute-done.19.refs_0_ = bf16[2,128,256]{2,1,0:T(8,128)(2,1)S(1)} collective-permute-done((bf16[2,128,256]{2,1,0:T(8,128)(2,1)S(1)}, bf16[2,128,256]{2,1,0:T(8,128)(2,1)S(1)}, u32[]{:S(2)}, u32[]{:S(2)}) %collective-permute-start.19) | collective-permute-done | bytes 131104 | tf_op jit(solution)/shard_map/ppermute | solution.py:285
  45.8 0.9 %collective-permute-done.21.refs_1_ = bf16[2,128,256]{2,1,0:T(8,128)(2,1)S(1)} collective-permute-done((bf16[2,128,256]{2,1,0:T(8,128)(2,1)S(1)}, bf16[2,128,256]{2,1,0:T(8,128)(2,1)S(1)}, u32[]{:S(2)}, u32[]{:S(2)}) %collective-permute-start.21) | collective-permute-done | bytes 131104 | tf_op jit(solution)/shard_map/ppermute | solution.py:285
  46.6 1.4 %collective-permute-done.23.refs_2_ = bf16[2,128,256]{2,1,0:T(8,128)(2,1)S(1)} collective-permute-done((bf16[2,128,256]{2,1,0:T(8,128)(2,1)S(1)}, bf16[2,128,256]{2,1,0:T(8,128)(2,1)S(1)}, u32[]{:S(2)}, u32[]{:S(2)}) %collective-permute-start.23) | collective-permute-done | bytes 131104 | tf_op jit(solution)/shard_map/ppermute | solution.py:285
  48.0 0.9 %collective-permute-done.25.refs_3_ = bf16[2,128,256]{2,1,0:T(8,128)(2,1)S(1)} collective-permute-done((bf16[2,128,256]{2,1,0:T(8,128)(2,1)S(1)}, bf16[2,128,256]{2,1,0:T(8,128)(2,1)S(1)}, u32[]{:S(2)}, u32[]{:S(2)}) %collective-permute-start.25) | collective-permute-done | bytes 131104 | tf_op jit(solution)/shard_map/ppermute | solution.py:285
  49.3 0.9 %collective-permute-done.26.refs_3_ = bf16[2,128,256]{2,1,0:T(8,128)(2,1)S(1)} collective-permute-done((bf16[2,128,256]{2,1,0:T(8,128)(2,1)S(1)}, bf16[2,128,256]{2,1,0:T(8,128)(2,1)S(1)}, u32[]{:S(2)}, u32[]{:S(2)}) %collective-permute-start.26) | collective-permute-done | bytes 131104 | tf_op jit(solution)/shard_map/ppermute | solution.py:269
  50.2 1.0 %shard_map.55 = bf16[512,256]{1,0:T(8,128)(2,1)} custom-call(s32[512,1]{1,0:T(8,128)S(1)} %shard_map.47.place_ref, bf16[2,128,256]{2,1,0:T(8,128)(2,1)S(1)} %collective-permute-done.20.refs_0_, bf16[2,128,256]{2,1,0:T(8,128)(2,1)S(1)} %collective-permute-done.22.refs_1_, bf16[2,128,256]{2,1,0:T(8,128)(2,1)S(1)} %collective-permute-done.24.refs_2_, ...), custom_call_target="tpu_custom_call" | custom-call | tf_op jit(solution)/shard_map/pallas_call | solution.py:252
  (43 shorter events, 5.8 us)
Async XLA Ops:
  1.2 4.2 %collective-permute-start.1 = (bf16[520,256]{1,0:T(8,128)(2,1)S(1)}, bf16[520,256]{1,0:T(8,128)(2,1)S(1)}, u32[]{:S(2)}, u32[]{:S(2)}) collective-permute-start(bf16[520,256]{1,0:T(8,128)(2,1)S(1)} %shard_map.46.refs_0_), channel_id=1, source_target_pairs={{0,4},{4,0},{1,5},{5,1},{2,6},{6,2},{3,7},{7,3},{8,12},{12,8},{9,1... | collective-permute-start | bytes 798728 | tf_op jit(solution)/shard_map/ppermute | solution.py:269
  1.7 16.5 %collective-permute-start = (bf16[520,256]{1,0:T(8,128)(2,1)S(1)}, bf16[520,256]{1,0:T(8,128)(2,1)S(1)}, u32[]{:S(2)}, u32[]{:S(2)}) collective-permute-start(bf16[520,256]{1,0:T(8,128)(2,1)S(1)} %shard_map.46.refs_0_), channel_id=1, source_target_pairs={{0,16},{16,0},{1,17},{17,1},{2,18},{18,2},{3,19},{19,3},{4,20},{20... | collective-permute-start | bytes 798728 | tf_op jit(solution)/shard_map/ppermute | solution.py:272
  6.3 11.8 %collective-permute-start.2 = (bf16[2,136,256]{2,1,0:T(8,128)(2,1)S(1)}, bf16[2,136,256]{2,1,0:T(8,128)(2,1)S(1)}, u32[]{:S(2)}, u32[]{:S(2)}) collective-permute-start(bf16[2,136,256]{2,1,0:T(8,128)(2,1)S(1)} %get-tuple-element.45), channel_id=1, source_target_pairs={{0,11},{4,13},{1,10},{5,12},{2,9},{6,15},{3,8},{7,14},{8,3},{12,5}... | collective-permute-start | bytes 417800 | tf_op jit(solution)/shard_map/ppermute | solution.py:285
  9.9 11.0 %collective-permute-start.3 = (bf16[2,136,256]{2,1,0:T(8,128)(2,1)S(1)}, bf16[2,136,256]{2,1,0:T(8,128)(2,1)S(1)}, u32[]{:S(2)}, u32[]{:S(2)}) collective-permute-start(bf16[2,136,256]{2,1,0:T(8,128)(2,1)S(1)} %get-tuple-element.46), channel_id=1, source_target_pairs={{0,8},{4,14},{1,9},{5,15},{2,10},{6,12},{3,11},{7,13},{8,0},{12,6}... | collective-permute-start | bytes 417800 | tf_op jit(solution)/shard_map/ppermute | solution.py:285
  10.3 10.5 %collective-permute-start.4 = (bf16[2,136,256]{2,1,0:T(8,128)(2,1)S(1)}, bf16[2,136,256]{2,1,0:T(8,128)(2,1)S(1)}, u32[]{:S(2)}, u32[]{:S(2)}) collective-permute-start(bf16[2,136,256]{2,1,0:T(8,128)(2,1)S(1)} %get-tuple-element.47), channel_id=1, source_target_pairs={{0,1},{4,7},{1,0},{5,6},{2,3},{6,5},{3,2},{7,4},{8,9},{12,15},{9,8... | collective-permute-start | bytes 417800 | tf_op jit(solution)/shard_map/ppermute | solution.py:285
  10.8 10.0 %collective-permute-start.5 = (bf16[2,136,256]{2,1,0:T(8,128)(2,1)S(1)}, bf16[2,136,256]{2,1,0:T(8,128)(2,1)S(1)}, u32[]{:S(2)}, u32[]{:S(2)}) collective-permute-start(bf16[2,136,256]{2,1,0:T(8,128)(2,1)S(1)} %get-tuple-element.48), channel_id=1, source_target_pairs={{0,6},{4,0},{1,7},{5,1},{2,4},{6,2},{3,5},{7,3},{8,14},{12,8},{9,1... | collective-permute-start | bytes 417800 | tf_op jit(solution)/shard_map/ppermute | solution.py:285
  20.9 2.6 %collective-permute-start.6 = (bf16[2,136,256]{2,1,0:T(8,128)(2,1)S(1)}, bf16[2,136,256]{2,1,0:T(8,128)(2,1)S(1)}, u32[]{:S(2)}, u32[]{:S(2)}) collective-permute-start(bf16[2,136,256]{2,1,0:T(8,128)(2,1)S(1)} %collective-permute-done.2.refs_0_.refs_4_), channel_id=1, source_target_pairs={{0,4},{4,0},{1,5},{5,1},{2,6},{6,2},{3,7},{7,3},{8,12},{12,8},{9,1... | collective-permute-start | bytes 417800 | tf_op jit(solution)/shard_map/ppermute | solution.py:269
  21.4 2.9 %collective-permute-start.7 = (bf16[2,136,256]{2,1,0:T(8,128)(2,1)S(1)}, bf16[2,136,256]{2,1,0:T(8,128)(2,1)S(1)}, u32[]{:S(2)}, u32[]{:S(2)}) collective-permute-start(bf16[2,136,256]{2,1,0:T(8,128)(2,1)S(1)} %collective-permute-done.3.refs_1_.refs_5_), channel_id=1, source_target_pairs={{0,4},{4,0},{1,5},{5,1},{2,6},{6,2},{3,7},{7,3},{8,12},{12,8},{9,1... | collective-permute-start | bytes 417800 | tf_op jit(solution)/shard_map/ppermute | solution.py:269
  21.4 4.4 %collective-permute-start.8 = (bf16[2,136,256]{2,1,0:T(8,128)(2,1)S(1)}, bf16[2,136,256]{2,1,0:T(8,128)(2,1)S(1)}, u32[]{:S(2)}, u32[]{:S(2)}) collective-permute-start(bf16[2,136,256]{2,1,0:T(8,128)(2,1)S(1)} %collective-permute-done.4.refs_2_.refs_6_.refs_0_), channel_id=1, source_target_pairs={{0,4},{4,0},{1,5},{5,1},{2,6},{6,2},{3,7},{7,3},{8,12},{12,8},{9,1... | collective-permute-start | bytes 417800 | tf_op jit(solution)/shard_map/ppermute | solution.py:269
  21.9 6.6 %collective-permute-start.9 = (bf16[2,136,256]{2,1,0:T(8,128)(2,1)S(1)}, bf16[2,136,256]{2,1,0:T(8,128)(2,1)S(1)}, u32[]{:S(2)}, u32[]{:S(2)}) collective-permute-start(bf16[2,136,256]{2,1,0:T(8,128)(2,1)S(1)} %collective-permute-done.5.refs_3_.refs_7_.refs_1_), channel_id=1, source_target_pairs={{0,4},{4,0},{1,5},{5,1},{2,6},{6,2},{3,7},{7,3},{8,12},{12,8},{9,1... | collective-permute-start | bytes 417800 | tf_op jit(solution)/shard_map/ppermute | solution.py:269
  23.4 8.9 %collective-permute-start.12 = (bf16[2,136,256]{2,1,0:T(8,128)(2,1)S(1)}, bf16[2,136,256]{2,1,0:T(8,128)(2,1)S(1)}, u32[]{:S(2)}, u32[]{:S(2)}) collective-permute-start(bf16[2,136,256]{2,1,0:T(8,128)(2,1)S(1)} %get-tuple-element.66), channel_id=1, source_target_pairs={{0,8},{4,14},{1,9},{5,15},{2,10},{6,12},{3,11},{7,13},{8,0},{12,6}... | collective-permute-start | bytes 417800 | tf_op jit(solution)/shard_map/ppermute | solution.py:285
  23.5 9.5 %collective-permute-start.13 = (bf16[2,136,256]{2,1,0:T(8,128)(2,1)S(1)}, bf16[2,136,256]{2,1,0:T(8,128)(2,1)S(1)}, u32[]{:S(2)}, u32[]{:S(2)}) collective-permute-start(bf16[2,136,256]{2,1,0:T(8,128)(2,1)S(1)} %get-tuple-element.67), channel_id=1, source_target_pairs={{0,1},{4,7},{1,0},{5,6},{2,3},{6,5},{3,2},{7,4},{8,9},{12,15},{9,8... | collective-permute-start | bytes 417800 | tf_op jit(solution)/shard_map/ppermute | solution.py:285
  24.2 8.8 %collective-permute-start.14 = (bf16[2,136,256]{2,1,0:T(8,128)(2,1)S(1)}, bf16[2,136,256]{2,1,0:T(8,128)(2,1)S(1)}, u32[]{:S(2)}, u32[]{:S(2)}) collective-permute-start(bf16[2,136,256]{2,1,0:T(8,128)(2,1)S(1)} %get-tuple-element.68), channel_id=1, source_target_pairs={{0,6},{4,0},{1,7},{5,1},{2,4},{6,2},{3,5},{7,3},{8,14},{12,8},{9,1... | collective-permute-start | bytes 417800 | tf_op jit(solution)/shard_map/ppermute | solution.py:285
  25.8 7.3 %collective-permute-start.11 = (bf16[2,136,256]{2,1,0:T(8,128)(2,1)S(1)}, bf16[2,136,256]{2,1,0:T(8,128)(2,1)S(1)}, u32[]{:S(2)}, u32[]{:S(2)}) collective-permute-start(bf16[2,136,256]{2,1,0:T(8,128)(2,1)S(1)} %get-tuple-element.55), channel_id=1, source_target_pairs={{0,11},{4,13},{1,10},{5,12},{2,9},{6,15},{3,8},{7,14},{8,3},{12,5}... | collective-permute-start | bytes 417800 | tf_op jit(solution)/shard_map/ppermute | solution.py:285
  33.1 3.1 %collective-permute-start.15 = (bf16[2,136,256]{2,1,0:T(8,128)(2,1)S(1)}, bf16[2,136,256]{2,1,0:T(8,128)(2,1)S(1)}, u32[]{:S(2)}, u32[]{:S(2)}) collective-permute-start(bf16[2,136,256]{2,1,0:T(8,128)(2,1)S(1)} %collective-permute-done.11.refs_6_), channel_id=1, source_target_pairs={{0,4},{4,0},{1,5},{5,1},{2,6},{6,2},{3,7},{7,3},{8,12},{12,8},{9,1... | collective-permute-start | bytes 417800 | tf_op jit(solution)/shard_map/ppermute | solution.py:269
  33.1 3.1 %collective-permute-start.16 = (bf16[2,136,256]{2,1,0:T(8,128)(2,1)S(1)}, bf16[2,136,256]{2,1,0:T(8,128)(2,1)S(1)}, u32[]{:S(2)}, u32[]{:S(2)}) collective-permute-start(bf16[2,136,256]{2,1,0:T(8,128)(2,1)S(1)} %collective-permute-done.12.refs_7_), channel_id=1, source_target_pairs={{0,4},{4,0},{1,5},{5,1},{2,6},{6,2},{3,7},{7,3},{8,12},{12,8},{9,1... | collective-permute-start | bytes 417800 | tf_op jit(solution)/shard_map/ppermute | solution.py:269
  33.6 2.6 %collective-permute-start.17 = (bf16[2,136,256]{2,1,0:T(8,128)(2,1)S(1)}, bf16[2,136,256]{2,1,0:T(8,128)(2,1)S(1)}, u32[]{:S(2)}, u32[]{:S(2)}) collective-permute-start(bf16[2,136,256]{2,1,0:T(8,128)(2,1)S(1)} %collective-permute-done.13.refs_8_), channel_id=1, source_target_pairs={{0,4},{4,0},{1,5},{5,1},{2,6},{6,2},{3,7},{7,3},{8,12},{12,8},{9,1... | collective-permute-start | bytes 417800 | tf_op jit(solution)/shard_map/ppermute | solution.py:269
  33.6 2.6 %collective-permute-start.18 = (bf16[2,136,256]{2,1,0:T(8,128)(2,1)S(1)}, bf16[2,136,256]{2,1,0:T(8,128)(2,1)S(1)}, u32[]{:S(2)}, u32[]{:S(2)}) collective-permute-start(bf16[2,136,256]{2,1,0:T(8,128)(2,1)S(1)} %collective-permute-done.14.refs_9_), channel_id=1, source_target_pairs={{0,4},{4,0},{1,5},{5,1},{2,6},{6,2},{3,7},{7,3},{8,12},{12,8},{9,1... | collective-permute-start | bytes 417800 | tf_op jit(solution)/shard_map/ppermute | solution.py:269
  37.5 8.2 %collective-permute-start.19 = (bf16[2,128,256]{2,1,0:T(8,128)(2,1)S(1)}, bf16[2,128,256]{2,1,0:T(8,128)(2,1)S(1)}, u32[]{:S(2)}, u32[]{:S(2)}) collective-permute-start(bf16[2,128,256]{2,1,0:T(8,128)(2,1)S(1)} %get-tuple-element.79), channel_id=1, source_target_pairs={{11,0},{13,4},{10,1},{12,5},{9,2},{15,6},{8,3},{14,7},{3,8},{5,12}... | collective-permute-start | bytes 393224 | tf_op jit(solution)/shard_map/ppermute | solution.py:285
  40.0 6.6 %collective-permute-start.21 = (bf16[2,128,256]{2,1,0:T(8,128)(2,1)S(1)}, bf16[2,128,256]{2,1,0:T(8,128)(2,1)S(1)}, u32[]{:S(2)}, u32[]{:S(2)}) collective-permute-start(bf16[2,128,256]{2,1,0:T(8,128)(2,1)S(1)} %get-tuple-element.80), channel_id=1, source_target_pairs={{8,0},{14,4},{9,1},{15,5},{10,2},{12,6},{11,3},{13,7},{0,8},{6,12}... | collective-permute-start | bytes 393224 | tf_op jit(solution)/shard_map/ppermute | solution.py:285
  42.4 5.5 %collective-permute-start.23 = (bf16[2,128,256]{2,1,0:T(8,128)(2,1)S(1)}, bf16[2,128,256]{2,1,0:T(8,128)(2,1)S(1)}, u32[]{:S(2)}, u32[]{:S(2)}) collective-permute-start(bf16[2,128,256]{2,1,0:T(8,128)(2,1)S(1)} %get-tuple-element.83), channel_id=1, source_target_pairs={{1,0},{7,4},{0,1},{6,5},{3,2},{5,6},{2,3},{4,7},{9,8},{15,12},{8,9... | collective-permute-start | bytes 393224 | tf_op jit(solution)/shard_map/ppermute | solution.py:285
  43.2 5.7 %collective-permute-start.25 = (bf16[2,128,256]{2,1,0:T(8,128)(2,1)S(1)}, bf16[2,128,256]{2,1,0:T(8,128)(2,1)S(1)}, u32[]{:S(2)}, u32[]{:S(2)}) collective-permute-start(bf16[2,128,256]{2,1,0:T(8,128)(2,1)S(1)} %get-tuple-element.84), channel_id=1, source_target_pairs={{6,0},{0,4},{7,1},{1,5},{4,2},{2,6},{5,3},{3,7},{14,8},{8,12},{15,... | collective-permute-start | bytes 393224 | tf_op jit(solution)/shard_map/ppermute | solution.py:285
  45.8 3.4 %collective-permute-start.20 = (bf16[2,128,256]{2,1,0:T(8,128)(2,1)S(1)}, bf16[2,128,256]{2,1,0:T(8,128)(2,1)S(1)}, u32[]{:S(2)}, u32[]{:S(2)}) collective-permute-start(bf16[2,128,256]{2,1,0:T(8,128)(2,1)S(1)} %collective-permute-done.19.refs_0_), channel_id=1, source_target_pairs={{0,4},{4,0},{1,5},{5,1},{2,6},{6,2},{3,7},{7,3},{8,12},{12,8},{9,1... | collective-permute-start | bytes 393224 | tf_op jit(solution)/shard_map/ppermute | solution.py:269
  46.6 2.6 %collective-permute-start.22 = (bf16[2,128,256]{2,1,0:T(8,128)(2,1)S(1)}, bf16[2,128,256]{2,1,0:T(8,128)(2,1)S(1)}, u32[]{:S(2)}, u32[]{:S(2)}) collective-permute-start(bf16[2,128,256]{2,1,0:T(8,128)(2,1)S(1)} %collective-permute-done.21.refs_1_), channel_id=1, source_target_pairs={{0,4},{4,0},{1,5},{5,1},{2,6},{6,2},{3,7},{7,3},{8,12},{12,8},{9,1... | collective-permute-start | bytes 393224 | tf_op jit(solution)/shard_map/ppermute | solution.py:269
  (4 other events, 5.6 us)

commit v4 on v3

--- a/solution.py
+++ b/solution.py
@@ -292,7 +292,12 @@
     block = scale(records, owner, subkey, source)
     far_block = to_half(block)
     places = place(owner, flips, cap)
-    held = [to_chip(m, j) for j, m in enumerate(pack((block, to_core(block)), flips, cap))]
+    half = chips // 4
+    pair = (block, to_core(block))
+    messages = pack(pair, [f[:half] for f in flips], cap)
+    pair, messages = lax.optimization_barrier((pair, messages))
+    messages = messages + pack(pair, [f[half:] for f in flips], cap)
+    held = [to_chip(m, j) for j, m in enumerate(messages)]
     far_block, places, held = lax.optimization_barrier((far_block, places, held))
     near_keys = gathered(held)
     near_keys = near_keys + [to_core(m) for m in near_keys]

time: 51.4 us -> 51.1 us (level)
  waiting for transfers between devices: 16.9 us -> 16.1 us
    ppermute x1, waiting for transfers between devices: 6.22 us -> 5.7 us  [to_half(): return lax.ppermute(x, 'z_hi', SWAP)]
    pallas_call x2 -> x3, Pallas kernels: 1.97 us -> 2.41 us  [pack(): pl.pallas_call(functools.partial(pack_kernel, flips, cap), in_specs=[pl.B...]
  transfers between devices with their start and end apart: 27 -> 27, of which waited for: 11 -> 10; matrix products, arithmetic and copies ran while one was open for 0% -> 0% of each run, Pallas kernels for 19% -> 20%
where the time goes in v4:
time: 51.1 us; the launch traced here: 50.9 us
  starting transfers between devices  20.7 us (41%)
  waiting for transfers between devices  16.1 us (32%)
  Pallas kernels  13.9 us (27%)
    ppermute x12, starting transfers between devices, to_chip(): return lax.ppermute(x, ('z_lo', 'core', 'near'), pairs)  14.4 us
    ppermute x12, waiting for transfers between devices, to_chip(): return lax.ppermute(x, ('z_lo', 'core', 'near'), pairs)  8.9 us
    pallas_call x4, Pallas kernels, match(): pl.pallas_call(functools.partial(match_kernel, count, cap, start, sums is...  8.42 us
    ppermute x1, waiting for transfers between devices, to_half(): return lax.ppermute(x, 'z_hi', SWAP)  5.7 us
    ppermute x1, starting transfers between devices, to_half(): return lax.ppermute(x, 'z_hi', SWAP)  3.66 us
    ppermute x14, starting transfers between devices, to_core(): return lax.ppermute(x, 'core', SWAP)  2.64 us
    pallas_call x3, Pallas kernels, pack(): pl.pallas_call(functools.partial(pack_kernel, flips, cap), in_specs=[pl.B...  2.41 us
    ppermute x14, waiting for transfers between devices, to_core(): return lax.ppermute(x, 'core', SWAP)  1.45 us
  transfers between devices with their start and end apart: 27, of which 10 were waited for; matrix products, arithmetic and copies ran while one was open for 0% of the time, Pallas kernels for 20%

profile of v4, /device:TPU:0, one launch (start us, length us, event | category | flops | bytes accessed | tf_op | source)
XLA Modules:
  0.0 50.9 jit_solution(5026042078484647198)
XLA Ops:
  0.0 1.1 %shard_map.46.refs_0_ = bf16[520,256]{1,0:T(8,128)(2,1)S(1)} custom-call(bf16[512,256]{1,0:T(8,128)(2,1)} %rows_hbm.1, s32[1,512]{1,0:T(1,128)} %bitcast.3, s32[1,512]{1,0:T(1,128)} %bitcast.4, s32[1,512]{1,0:T(1,128)} %bitcast.5), custom_call_target="tpu_custom_call" | custom-call | tf_op jit(solution)/shard_map/pallas_call | solution.py:76
  1.7 3.7 %collective-permute-start = (bf16[520,256]{1,0:T(8,128)(2,1)S(1)}, bf16[520,256]{1,0:T(8,128)(2,1)S(1)}, u32[]{:S(2)}, u32[]{:S(2)}) collective-permute-start(bf16[520,256]{1,0:T(8,128)(2,1)S(1)} %shard_map.46.refs_0_), channel_id=1, source_target_pairs={{0,16},{16,0},{1,17},{17,1},{2,18},{18,2},{3,19},{19,3},{4,20},{20... | collective-permute-start | bytes 798728 | tf_op jit(solution)/shard_map/ppermute | solution.py:272
  5.3 0.7 %shard_map.48 = (bf16[2,136,256]{2,1,0:T(8,128)(2,1)S(1)}, bf16[2,136,256]{2,1,0:T(8,128)(2,1)S(1)}) custom-call(bf16[520,256]{1,0:T(8,128)(2,1)S(1)} %shard_map.46.refs_0_, bf16[520,256]{1,0:T(8,128)(2,1)S(1)} %collective-permute-done.1.refs_1_), custom_call_target="tpu_custom_call" | custom-call | tf_op jit(solution)/shard_map/pallas_call | solution.py:121
  6.1 3.5 %collective-permute-start.2 = (bf16[2,136,256]{2,1,0:T(8,128)(2,1)S(1)}, bf16[2,136,256]{2,1,0:T(8,128)(2,1)S(1)}, u32[]{:S(2)}, u32[]{:S(2)}) collective-permute-start(bf16[2,136,256]{2,1,0:T(8,128)(2,1)S(1)} %get-tuple-element.51), channel_id=1, source_target_pairs={{0,11},{4,13},{1,10},{5,12},{2,9},{6,15},{3,8},{7,14},{8,3},{12,5}... | collective-permute-start | bytes 417800 | tf_op jit(solution)/shard_map/ppermute | solution.py:285
  10.0 0.7 %shard_map.49 = (bf16[2,136,256]{2,1,0:T(8,128)(2,1)S(1)}, bf16[2,136,256]{2,1,0:T(8,128)(2,1)S(1)}) custom-call(bf16[520,256]{1,0:T(8,128)(2,1)S(1)} %shard_map.46.refs_0_, bf16[520,256]{1,0:T(8,128)(2,1)S(1)} %collective-permute-done.1.refs_1_), custom_call_target="tpu_custom_call" | custom-call | tf_op jit(solution)/shard_map/pallas_call | solution.py:121
  12.4 5.7 %collective-permute-done.refs_0_ = bf16[520,256]{1,0:T(8,128)(2,1)S(1)} collective-permute-done((bf16[520,256]{1,0:T(8,128)(2,1)S(1)}, bf16[520,256]{1,0:T(8,128)(2,1)S(1)}, u32[]{:S(2)}, u32[]{:S(2)}) %collective-permute-start) | collective-permute-done | bytes 266272 | tf_op jit(solution)/shard_map/ppermute | solution.py:272
  18.1 2.4 %collective-permute-done.3.refs_1_.refs_5_ = bf16[2,136,256]{2,1,0:T(8,128)(2,1)S(1)} collective-permute-done((bf16[2,136,256]{2,1,0:T(8,128)(2,1)S(1)}, bf16[2,136,256]{2,1,0:T(8,128)(2,1)S(1)}, u32[]{:S(2)}, u32[]{:S(2)}) %collective-permute-start.3) | collective-permute-done | bytes 139296 | tf_op jit(solution)/shard_map/ppermute | solution.py:285
  22.1 1.0 %shard_map.50 = (bf16[2,136,256]{2,1,0:T(8,128)(2,1)S(1)}, bf16[2,136,256]{2,1,0:T(8,128)(2,1)S(1)}, bf16[2,136,256]{2,1,0:T(8,128)(2,1)S(1)}, bf16[2,136,256]{2,1,0:T(8,128)(2,1)S(1)}) custom-call(bf16[520,256]{1,0:T(8,128)(2,1)S(1)} %collective-permute-done.refs_0_, bf16[520,256]{1,0:T(8,128)(2,1)S(1)} %collective-permute-done.10.refs_1_), custom_call_target="tpu_custom_call" | custom-call | tf_op jit(solution)/shard_map/pallas_call | solution.py:121
  23.4 1.2 %collective-permute-start.13 = (bf16[2,136,256]{2,1,0:T(8,128)(2,1)S(1)}, bf16[2,136,256]{2,1,0:T(8,128)(2,1)S(1)}, u32[]{:S(2)}, u32[]{:S(2)}) collective-permute-start(bf16[2,136,256]{2,1,0:T(8,128)(2,1)S(1)} %get-tuple-element.75), channel_id=1, source_target_pairs={{0,1},{4,7},{1,0},{5,6},{2,3},{6,5},{3,2},{7,4},{8,9},{12,15},{9,8... | collective-permute-start | bytes 417800 | tf_op jit(solution)/shard_map/ppermute | solution.py:285
  24.5 1.3 %collective-permute-start.14 = (bf16[2,136,256]{2,1,0:T(8,128)(2,1)S(1)}, bf16[2,136,256]{2,1,0:T(8,128)(2,1)S(1)}, u32[]{:S(2)}, u32[]{:S(2)}) collective-permute-start(bf16[2,136,256]{2,1,0:T(8,128)(2,1)S(1)} %get-tuple-element.76), channel_id=1, source_target_pairs={{0,6},{4,0},{1,7},{5,1},{2,4},{6,2},{3,5},{7,3},{8,14},{12,8},{9,1... | collective-permute-start | bytes 417800 | tf_op jit(solution)/shard_map/ppermute | solution.py:285
  25.8 2.4 %collective-permute-start.11 = (bf16[2,136,256]{2,1,0:T(8,128)(2,1)S(1)}, bf16[2,136,256]{2,1,0:T(8,128)(2,1)S(1)}, u32[]{:S(2)}, u32[]{:S(2)}) collective-permute-start(bf16[2,136,256]{2,1,0:T(8,128)(2,1)S(1)} %get-tuple-element.63), channel_id=1, source_target_pairs={{0,11},{4,13},{1,10},{5,12},{2,9},{6,15},{3,8},{7,14},{8,3},{12,5}... | collective-permute-start | bytes 417800 | tf_op jit(solution)/shard_map/ppermute | solution.py:285
  28.2 3.9 %shard_map.51 = (f32[1024,256]{1,0:T(8,128)S(1)}, f32[1024,1]{1,0:T(8,128)S(1)}) custom-call(bf16[2,136,256]{2,1,0:T(8,128)(2,1)S(1)} %collective-permute-done.2.refs_0_.refs_4_, bf16[2,136,256]{2,1,0:T(8,128)(2,1)S(1)} %collective-permute-done.3.refs_1_.refs_5_, bf16[2,136,256]{2,1,0:T(8,128)(2,1)S(1)} %collective-permute-done.4.refs_2_.refs_6_.refs_0_, ...), custom_call_target="tpu_custom_call" | custom-call | tf_op jit(solution)/shard_map/pallas_call | solution.py:228
  32.1 0.8 %collective-permute-done.13.refs_8_ = bf16[2,136,256]{2,1,0:T(8,128)(2,1)S(1)} collective-permute-done((bf16[2,136,256]{2,1,0:T(8,128)(2,1)S(1)}, bf16[2,136,256]{2,1,0:T(8,128)(2,1)S(1)}, u32[]{:S(2)}, u32[]{:S(2)}) %collective-permute-start.13) | collective-permute-done | bytes 139296 | tf_op jit(solution)/shard_map/ppermute | solution.py:285
  33.9 2.1 %shard_map.52 = (f32[1024,256]{1,0:T(8,128)S(1)}, f32[1024,1]{1,0:T(8,128)S(1)}) custom-call(bf16[2,136,256]{2,1,0:T(8,128)(2,1)S(1)} %collective-permute-done.2.refs_0_.refs_4_, bf16[2,136,256]{2,1,0:T(8,128)(2,1)S(1)} %collective-permute-done.3.refs_1_.refs_5_, bf16[2,136,256]{2,1,0:T(8,128)(2,1)S(1)} %collective-permute-done.4.refs_2_.refs_6_.refs_0_, ...), custom_call_target="tpu_custom_call" | custom-call | tf_op jit(solution)/shard_map/pallas_call | solution.py:228
  36.0 1.3 %shard_map.53 = (bf16[2,128,256]{2,1,0:T(8,128)(2,1)S(1)}, bf16[2,128,256]{2,1,0:T(8,128)(2,1)S(1)}) custom-call(bf16[2,136,256]{2,1,0:T(8,128)(2,1)S(1)} %collective-permute-done.2.refs_0_.refs_4_, bf16[2,136,256]{2,1,0:T(8,128)(2,1)S(1)} %collective-permute-done.3.refs_1_.refs_5_, f32[1024,256]{1,0:T(8,128)S(1)} %get-tuple-element.89.refs_2_, ...), custom_call_target="tpu_custom_call" | custom-call | tf_op jit(solution)/shard_map/pallas_call | solution.py:228
  37.3 2.4 %collective-permute-start.19 = (bf16[2,128,256]{2,1,0:T(8,128)(2,1)S(1)}, bf16[2,128,256]{2,1,0:T(8,128)(2,1)S(1)}, u32[]{:S(2)}, u32[]{:S(2)}) collective-permute-start(bf16[2,128,256]{2,1,0:T(8,128)(2,1)S(1)} %get-tuple-element.87), channel_id=1, source_target_pairs={{11,0},{13,4},{10,1},{12,5},{9,2},{15,6},{8,3},{14,7},{3,8},{5,12}... | collective-permute-start | bytes 393224 | tf_op jit(solution)/shard_map/ppermute | solution.py:285
  39.7 1.2 %collective-permute-start.21 = (bf16[2,128,256]{2,1,0:T(8,128)(2,1)S(1)}, bf16[2,128,256]{2,1,0:T(8,128)(2,1)S(1)}, u32[]{:S(2)}, u32[]{:S(2)}) collective-permute-start(bf16[2,128,256]{2,1,0:T(8,128)(2,1)S(1)} %get-tuple-element.88), channel_id=1, source_target_pairs={{8,0},{14,4},{9,1},{15,5},{10,2},{12,6},{11,3},{13,7},{0,8},{6,12}... | collective-permute-start | bytes 393224 | tf_op jit(solution)/shard_map/ppermute | solution.py:285
  40.9 1.3 %shard_map.54 = (bf16[2,128,256]{2,1,0:T(8,128)(2,1)S(1)}, bf16[2,128,256]{2,1,0:T(8,128)(2,1)S(1)}) custom-call(bf16[2,136,256]{2,1,0:T(8,128)(2,1)S(1)} %collective-permute-done.4.refs_2_.refs_6_.refs_0_, bf16[2,136,256]{2,1,0:T(8,128)(2,1)S(1)} %collective-permute-done.5.refs_3_.refs_7_.refs_1_, f32[1024,256]{1,0:T(8,128)S(1)} %get-tuple-element.89.refs_2_, ...), custom_call_target="tpu_custom_call" | custom-call | tf_op jit(solution)/shard_map/pallas_call | solution.py:228
  42.9 2.8 %collective-permute-done.19.refs_0_ = bf16[2,128,256]{2,1,0:T(8,128)(2,1)S(1)} collective-permute-done((bf16[2,128,256]{2,1,0:T(8,128)(2,1)S(1)}, bf16[2,128,256]{2,1,0:T(8,128)(2,1)S(1)}, u32[]{:S(2)}, u32[]{:S(2)}) %collective-permute-start.19) | collective-permute-done | bytes 131104 | tf_op jit(solution)/shard_map/ppermute | solution.py:285
  45.6 0.8 %collective-permute-done.21.refs_1_ = bf16[2,128,256]{2,1,0:T(8,128)(2,1)S(1)} collective-permute-done((bf16[2,128,256]{2,1,0:T(8,128)(2,1)S(1)}, bf16[2,128,256]{2,1,0:T(8,128)(2,1)S(1)}, u32[]{:S(2)}, u32[]{:S(2)}) %collective-permute-start.21) | collective-permute-done | bytes 131104 | tf_op jit(solution)/shard_map/ppermute | solution.py:285
  46.5 1.3 %collective-permute-done.23.refs_2_ = bf16[2,128,256]{2,1,0:T(8,128)(2,1)S(1)} collective-permute-done((bf16[2,128,256]{2,1,0:T(8,128)(2,1)S(1)}, bf16[2,128,256]{2,1,0:T(8,128)(2,1)S(1)}, u32[]{:S(2)}, u32[]{:S(2)}) %collective-permute-start.23) | collective-permute-done | bytes 131104 | tf_op jit(solution)/shard_map/ppermute | solution.py:285
  47.8 0.8 %collective-permute-done.25.refs_3_ = bf16[2,128,256]{2,1,0:T(8,128)(2,1)S(1)} collective-permute-done((bf16[2,128,256]{2,1,0:T(8,128)(2,1)S(1)}, bf16[2,128,256]{2,1,0:T(8,128)(2,1)S(1)}, u32[]{:S(2)}, u32[]{:S(2)}) %collective-permute-start.25) | collective-permute-done | bytes 131104 | tf_op jit(solution)/shard_map/ppermute | solution.py:285
  49.1 0.8 %collective-permute-done.26.refs_3_ = bf16[2,128,256]{2,1,0:T(8,128)(2,1)S(1)} collective-permute-done((bf16[2,128,256]{2,1,0:T(8,128)(2,1)S(1)}, bf16[2,128,256]{2,1,0:T(8,128)(2,1)S(1)}, u32[]{:S(2)}, u32[]{:S(2)}) %collective-permute-start.26) | collective-permute-done | bytes 131104 | tf_op jit(solution)/shard_map/ppermute | solution.py:269
  49.9 1.0 %shard_map.56 = bf16[512,256]{1,0:T(8,128)(2,1)} custom-call(s32[512,1]{1,0:T(8,128)S(1)} %shard_map.47.place_ref, bf16[2,128,256]{2,1,0:T(8,128)(2,1)S(1)} %collective-permute-done.20.refs_0_, bf16[2,128,256]{2,1,0:T(8,128)(2,1)S(1)} %collective-permute-done.22.refs_1_, bf16[2,128,256]{2,1,0:T(8,128)(2,1)S(1)} %collective-permute-done.24.refs_2_, ...), custom_call_target="tpu_custom_call" | custom-call | tf_op jit(solution)/shard_map/pallas_call | solution.py:252
  (44 shorter events, 6.8 us)
Async XLA Ops:
  1.2 4.2 %collective-permute-start.1 = (bf16[520,256]{1,0:T(8,128)(2,1)S(1)}, bf16[520,256]{1,0:T(8,128)(2,1)S(1)}, u32[]{:S(2)}, u32[]{:S(2)}) collective-permute-start(bf16[520,256]{1,0:T(8,128)(2,1)S(1)} %shard_map.46.refs_0_), channel_id=1, source_target_pairs={{0,4},{4,0},{1,5},{5,1},{2,6},{6,2},{3,7},{7,3},{8,12},{12,8},{9,1... | collective-permute-start | bytes 798728 | tf_op jit(solution)/shard_map/ppermute | solution.py:269
  1.7 16.5 %collective-permute-start = (bf16[520,256]{1,0:T(8,128)(2,1)S(1)}, bf16[520,256]{1,0:T(8,128)(2,1)S(1)}, u32[]{:S(2)}, u32[]{:S(2)}) collective-permute-start(bf16[520,256]{1,0:T(8,128)(2,1)S(1)} %shard_map.46.refs_0_), channel_id=1, source_target_pairs={{0,16},{16,0},{1,17},{17,1},{2,18},{18,2},{3,19},{19,3},{4,20},{20... | collective-permute-start | bytes 798728 | tf_op jit(solution)/shard_map/ppermute | solution.py:272
  6.1 12.1 %collective-permute-start.2 = (bf16[2,136,256]{2,1,0:T(8,128)(2,1)S(1)}, bf16[2,136,256]{2,1,0:T(8,128)(2,1)S(1)}, u32[]{:S(2)}, u32[]{:S(2)}) collective-permute-start(bf16[2,136,256]{2,1,0:T(8,128)(2,1)S(1)} %get-tuple-element.51), channel_id=1, source_target_pairs={{0,11},{4,13},{1,10},{5,12},{2,9},{6,15},{3,8},{7,14},{8,3},{12,5}... | collective-permute-start | bytes 417800 | tf_op jit(solution)/shard_map/ppermute | solution.py:285
  9.6 11.0 %collective-permute-start.3 = (bf16[2,136,256]{2,1,0:T(8,128)(2,1)S(1)}, bf16[2,136,256]{2,1,0:T(8,128)(2,1)S(1)}, u32[]{:S(2)}, u32[]{:S(2)}) collective-permute-start(bf16[2,136,256]{2,1,0:T(8,128)(2,1)S(1)} %get-tuple-element.52), channel_id=1, source_target_pairs={{0,8},{4,14},{1,9},{5,15},{2,10},{6,12},{3,11},{7,13},{8,0},{12,6}... | collective-permute-start | bytes 417800 | tf_op jit(solution)/shard_map/ppermute | solution.py:285
  10.8 9.8 %collective-permute-start.4 = (bf16[2,136,256]{2,1,0:T(8,128)(2,1)S(1)}, bf16[2,136,256]{2,1,0:T(8,128)(2,1)S(1)}, u32[]{:S(2)}, u32[]{:S(2)}) collective-permute-start(bf16[2,136,256]{2,1,0:T(8,128)(2,1)S(1)} %get-tuple-element.55), channel_id=1, source_target_pairs={{0,1},{4,7},{1,0},{5,6},{2,3},{6,5},{3,2},{7,4},{8,9},{12,15},{9,8... | collective-permute-start | bytes 417800 | tf_op jit(solution)/shard_map/ppermute | solution.py:285
  11.4 9.2 %collective-permute-start.5 = (bf16[2,136,256]{2,1,0:T(8,128)(2,1)S(1)}, bf16[2,136,256]{2,1,0:T(8,128)(2,1)S(1)}, u32[]{:S(2)}, u32[]{:S(2)}) collective-permute-start(bf16[2,136,256]{2,1,0:T(8,128)(2,1)S(1)} %get-tuple-element.56), channel_id=1, source_target_pairs={{0,6},{4,0},{1,7},{5,1},{2,4},{6,2},{3,5},{7,3},{8,14},{12,8},{9,1... | collective-permute-start | bytes 417800 | tf_op jit(solution)/shard_map/ppermute | solution.py:285
  20.6 2.8 %collective-permute-start.6 = (bf16[2,136,256]{2,1,0:T(8,128)(2,1)S(1)}, bf16[2,136,256]{2,1,0:T(8,128)(2,1)S(1)}, u32[]{:S(2)}, u32[]{:S(2)}) collective-permute-start(bf16[2,136,256]{2,1,0:T(8,128)(2,1)S(1)} %collective-permute-done.2.refs_0_.refs_4_), channel_id=1, source_target_pairs={{0,4},{4,0},{1,5},{5,1},{2,6},{6,2},{3,7},{7,3},{8,12},{12,8},{9,1... | collective-permute-start | bytes 417800 | tf_op jit(solution)/shard_map/ppermute | solution.py:269
  21.1 3.5 %collective-permute-start.7 = (bf16[2,136,256]{2,1,0:T(8,128)(2,1)S(1)}, bf16[2,136,256]{2,1,0:T(8,128)(2,1)S(1)}, u32[]{:S(2)}, u32[]{:S(2)}) collective-permute-start(bf16[2,136,256]{2,1,0:T(8,128)(2,1)S(1)} %collective-permute-done.3.refs_1_.refs_5_), channel_id=1, source_target_pairs={{0,4},{4,0},{1,5},{5,1},{2,6},{6,2},{3,7},{7,3},{8,12},{12,8},{9,1... | collective-permute-start | bytes 417800 | tf_op jit(solution)/shard_map/ppermute | solution.py:269
  21.2 4.7 %collective-permute-start.8 = (bf16[2,136,256]{2,1,0:T(8,128)(2,1)S(1)}, bf16[2,136,256]{2,1,0:T(8,128)(2,1)S(1)}, u32[]{:S(2)}, u32[]{:S(2)}) collective-permute-start(bf16[2,136,256]{2,1,0:T(8,128)(2,1)S(1)} %collective-permute-done.4.refs_2_.refs_6_.refs_0_), channel_id=1, source_target_pairs={{0,4},{4,0},{1,5},{5,1},{2,6},{6,2},{3,7},{7,3},{8,12},{12,8},{9,1... | collective-permute-start | bytes 417800 | tf_op jit(solution)/shard_map/ppermute | solution.py:269
  21.6 6.6 %collective-permute-start.9 = (bf16[2,136,256]{2,1,0:T(8,128)(2,1)S(1)}, bf16[2,136,256]{2,1,0:T(8,128)(2,1)S(1)}, u32[]{:S(2)}, u32[]{:S(2)}) collective-permute-start(bf16[2,136,256]{2,1,0:T(8,128)(2,1)S(1)} %collective-permute-done.5.refs_3_.refs_7_.refs_1_), channel_id=1, source_target_pairs={{0,4},{4,0},{1,5},{5,1},{2,6},{6,2},{3,7},{7,3},{8,12},{12,8},{9,1... | collective-permute-start | bytes 417800 | tf_op jit(solution)/shard_map/ppermute | solution.py:269
  23.1 9.0 %collective-permute-start.12 = (bf16[2,136,256]{2,1,0:T(8,128)(2,1)S(1)}, bf16[2,136,256]{2,1,0:T(8,128)(2,1)S(1)}, u32[]{:S(2)}, u32[]{:S(2)}) collective-permute-start(bf16[2,136,256]{2,1,0:T(8,128)(2,1)S(1)} %get-tuple-element.74), channel_id=1, source_target_pairs={{0,8},{4,14},{1,9},{5,15},{2,10},{6,12},{3,11},{7,13},{8,0},{12,6}... | collective-permute-start | bytes 417800 | tf_op jit(solution)/shard_map/ppermute | solution.py:285
  23.4 9.5 %collective-permute-start.13 = (bf16[2,136,256]{2,1,0:T(8,128)(2,1)S(1)}, bf16[2,136,256]{2,1,0:T(8,128)(2,1)S(1)}, u32[]{:S(2)}, u32[]{:S(2)}) collective-permute-start(bf16[2,136,256]{2,1,0:T(8,128)(2,1)S(1)} %get-tuple-element.75), channel_id=1, source_target_pairs={{0,1},{4,7},{1,0},{5,6},{2,3},{6,5},{3,2},{7,4},{8,9},{12,15},{9,8... | collective-permute-start | bytes 417800 | tf_op jit(solution)/shard_map/ppermute | solution.py:285
  24.5 8.4 %collective-permute-start.14 = (bf16[2,136,256]{2,1,0:T(8,128)(2,1)S(1)}, bf16[2,136,256]{2,1,0:T(8,128)(2,1)S(1)}, u32[]{:S(2)}, u32[]{:S(2)}) collective-permute-start(bf16[2,136,256]{2,1,0:T(8,128)(2,1)S(1)} %get-tuple-element.76), channel_id=1, source_target_pairs={{0,6},{4,0},{1,7},{5,1},{2,4},{6,2},{3,5},{7,3},{8,14},{12,8},{9,1... | collective-permute-start | bytes 417800 | tf_op jit(solution)/shard_map/ppermute | solution.py:285
  25.8 7.1 %collective-permute-start.11 = (bf16[2,136,256]{2,1,0:T(8,128)(2,1)S(1)}, bf16[2,136,256]{2,1,0:T(8,128)(2,1)S(1)}, u32[]{:S(2)}, u32[]{:S(2)}) collective-permute-start(bf16[2,136,256]{2,1,0:T(8,128)(2,1)S(1)} %get-tuple-element.63), channel_id=1, source_target_pairs={{0,11},{4,13},{1,10},{5,12},{2,9},{6,15},{3,8},{7,14},{8,3},{12,5}... | collective-permute-start | bytes 417800 | tf_op jit(solution)/shard_map/ppermute | solution.py:285
  32.9 3.1 %collective-permute-start.15 = (bf16[2,136,256]{2,1,0:T(8,128)(2,1)S(1)}, bf16[2,136,256]{2,1,0:T(8,128)(2,1)S(1)}, u32[]{:S(2)}, u32[]{:S(2)}) collective-permute-start(bf16[2,136,256]{2,1,0:T(8,128)(2,1)S(1)} %collective-permute-done.11.refs_6_), channel_id=1, source_target_pairs={{0,4},{4,0},{1,5},{5,1},{2,6},{6,2},{3,7},{7,3},{8,12},{12,8},{9,1... | collective-permute-start | bytes 417800 | tf_op jit(solution)/shard_map/ppermute | solution.py:269
  33.1 2.9 %collective-permute-start.16 = (bf16[2,136,256]{2,1,0:T(8,128)(2,1)S(1)}, bf16[2,136,256]{2,1,0:T(8,128)(2,1)S(1)}, u32[]{:S(2)}, u32[]{:S(2)}) collective-permute-start(bf16[2,136,256]{2,1,0:T(8,128)(2,1)S(1)} %collective-permute-done.12.refs_7_), channel_id=1, source_target_pairs={{0,4},{4,0},{1,5},{5,1},{2,6},{6,2},{3,7},{7,3},{8,12},{12,8},{9,1... | collective-permute-start | bytes 417800 | tf_op jit(solution)/shard_map/ppermute | solution.py:269
  33.4 2.6 %collective-permute-start.17 = (bf16[2,136,256]{2,1,0:T(8,128)(2,1)S(1)}, bf16[2,136,256]{2,1,0:T(8,128)(2,1)S(1)}, u32[]{:S(2)}, u32[]{:S(2)}) collective-permute-start(bf16[2,136,256]{2,1,0:T(8,128)(2,1)S(1)} %collective-permute-done.13.refs_8_), channel_id=1, source_target_pairs={{0,4},{4,0},{1,5},{5,1},{2,6},{6,2},{3,7},{7,3},{8,12},{12,8},{9,1... | collective-permute-start | bytes 417800 | tf_op jit(solution)/shard_map/ppermute | solution.py:269
  33.6 2.4 %collective-permute-start.18 = (bf16[2,136,256]{2,1,0:T(8,128)(2,1)S(1)}, bf16[2,136,256]{2,1,0:T(8,128)(2,1)S(1)}, u32[]{:S(2)}, u32[]{:S(2)}) collective-permute-start(bf16[2,136,256]{2,1,0:T(8,128)(2,1)S(1)} %collective-permute-done.14.refs_9_), channel_id=1, source_target_pairs={{0,4},{4,0},{1,5},{5,1},{2,6},{6,2},{3,7},{7,3},{8,12},{12,8},{9,1... | collective-permute-start | bytes 417800 | tf_op jit(solution)/shard_map/ppermute | solution.py:269
  37.3 8.3 %collective-permute-start.19 = (bf16[2,128,256]{2,1,0:T(8,128)(2,1)S(1)}, bf16[2,128,256]{2,1,0:T(8,128)(2,1)S(1)}, u32[]{:S(2)}, u32[]{:S(2)}) collective-permute-start(bf16[2,128,256]{2,1,0:T(8,128)(2,1)S(1)} %get-tuple-element.87), channel_id=1, source_target_pairs={{11,0},{13,4},{10,1},{12,5},{9,2},{15,6},{8,3},{14,7},{3,8},{5,12}... | collective-permute-start | bytes 393224 | tf_op jit(solution)/shard_map/ppermute | solution.py:285
  39.7 6.7 %collective-permute-start.21 = (bf16[2,128,256]{2,1,0:T(8,128)(2,1)S(1)}, bf16[2,128,256]{2,1,0:T(8,128)(2,1)S(1)}, u32[]{:S(2)}, u32[]{:S(2)}) collective-permute-start(bf16[2,128,256]{2,1,0:T(8,128)(2,1)S(1)} %get-tuple-element.88), channel_id=1, source_target_pairs={{8,0},{14,4},{9,1},{15,5},{10,2},{12,6},{11,3},{13,7},{0,8},{6,12}... | collective-permute-start | bytes 393224 | tf_op jit(solution)/shard_map/ppermute | solution.py:285
  42.2 5.6 %collective-permute-start.23 = (bf16[2,128,256]{2,1,0:T(8,128)(2,1)S(1)}, bf16[2,128,256]{2,1,0:T(8,128)(2,1)S(1)}, u32[]{:S(2)}, u32[]{:S(2)}) collective-permute-start(bf16[2,128,256]{2,1,0:T(8,128)(2,1)S(1)} %get-tuple-element.91), channel_id=1, source_target_pairs={{1,0},{7,4},{0,1},{6,5},{3,2},{5,6},{2,3},{4,7},{9,8},{15,12},{8,9... | collective-permute-start | bytes 393224 | tf_op jit(solution)/shard_map/ppermute | solution.py:285
  42.9 5.6 %collective-permute-start.25 = (bf16[2,128,256]{2,1,0:T(8,128)(2,1)S(1)}, bf16[2,128,256]{2,1,0:T(8,128)(2,1)S(1)}, u32[]{:S(2)}, u32[]{:S(2)}) collective-permute-start(bf16[2,128,256]{2,1,0:T(8,128)(2,1)S(1)} %get-tuple-element.92), channel_id=1, source_target_pairs={{6,0},{0,4},{7,1},{1,5},{4,2},{2,6},{5,3},{3,7},{14,8},{8,12},{15,... | collective-permute-start | bytes 393224 | tf_op jit(solution)/shard_map/ppermute | solution.py:285
  45.6 3.2 %collective-permute-start.20 = (bf16[2,128,256]{2,1,0:T(8,128)(2,1)S(1)}, bf16[2,128,256]{2,1,0:T(8,128)(2,1)S(1)}, u32[]{:S(2)}, u32[]{:S(2)}) collective-permute-start(bf16[2,128,256]{2,1,0:T(8,128)(2,1)S(1)} %collective-permute-done.19.refs_0_), channel_id=1, source_target_pairs={{0,4},{4,0},{1,5},{5,1},{2,6},{6,2},{3,7},{7,3},{8,12},{12,8},{9,1... | collective-permute-start | bytes 393224 | tf_op jit(solution)/shard_map/ppermute | solution.py:269
  46.5 2.4 %collective-permute-start.22 = (bf16[2,128,256]{2,1,0:T(8,128)(2,1)S(1)}, bf16[2,128,256]{2,1,0:T(8,128)(2,1)S(1)}, u32[]{:S(2)}, u32[]{:S(2)}) collective-permute-start(bf16[2,128,256]{2,1,0:T(8,128)(2,1)S(1)} %collective-permute-done.21.refs_1_), channel_id=1, source_target_pairs={{0,4},{4,0},{1,5},{5,1},{2,6},{6,2},{3,7},{7,3},{8,12},{12,8},{9,1... | collective-permute-start | bytes 393224 | tf_op jit(solution)/shard_map/ppermute | solution.py:269
  (4 other events, 5.2 us)
